TPU v7x, 32 devices: a whole 2x2x4 slice. The times are simulated.
32 devices in a mesh: groups: 2 (over y), seq: 4 (over z), mp: 2 (over x), rep: 2 (over core).
Axes of the slice: x: 2, y: 2, z: 4, core: 2. Of those that a mesh axis runs over, the one named last changes fastest.
Arguments:
- tokens: bfloat16 [8192, 2240], P(('groups', 'seq', 'rep')), parts along dimension 0, may hold values from -8 to 8
- slot_image: int32 [32], P(('groups', 'seq', 'rep')), parts along dimension 0, may hold values from 0 to 5, as said below
- modulation: float32 [12, 3, 2240], P('groups'), parts along dimension 0, may hold values from -3 to 3
- w_qkv: bfloat16 [2240, 3, 1280], P('rep', None, 'mp'), may hold values from -0.125 to 0.125
- w_out: bfloat16 [1280, 2240], P('rep', 'mp'), may hold values from -0.15625 to 0.15625
Outputs:
- updated: bfloat16 [8192, 2240], P(('groups', 'seq', 'rep'), 'mp'), parts along dimension 0
There are 2 independent parts, one for each index of `groups`. A program takes and returns all parts, laid end to end along the dimension named above; an argument that names none is the same for every part. Nothing has to cross between parts.
Inputs may be any that keep to these rules, and one draw needn't show every extreme that they name: `slot_image`: every one of the 6 images owns one tile slot or more.
All inputs are finite; a program needn't handle non-finite values.
Results may differ from a plain program's by a relative error of at most 0.0036.
Values may be sent and summed in bfloat16 or wider, within the bound.
No kernel may reach another device: no remote copies, remote signals or barrier semaphores. Data moves between devices by JAX's collectives and lax.ppermute only.
A program may use at most 128 MiB of HBM per device.

v0:
```python
import functools

import jax
import jax.numpy as jnp
from jax import lax
from jax.experimental import pallas as pl
from jax.experimental.pallas import tpu as pltpu
from jax.sharding import PartitionSpec as P

HD = 32
F32 = jnp.float32
BF16 = jnp.bfloat16
VM = pl.BlockSpec(memory_space=pltpu.VMEM)
HB = pl.BlockSpec(memory_space=pltpu.HBM)
MIB = 1 << 20


def call(kernel, out_shape, in_specs, out_specs=None, scratch=(), vmem=16, aliases=None, flops=0, nbytes=0):
    if out_specs is None:
        out_specs = [VM] * len(out_shape) if isinstance(out_shape, list) else VM
    return pl.pallas_call(
        kernel,
        out_shape=out_shape,
        in_specs=in_specs,
        out_specs=out_specs,
        scratch_shapes=list(scratch),
        input_output_aliases=aliases or {},
        compiler_params=pltpu.CompilerParams(vmem_limit_bytes=vmem * MIB),
        cost_estimate=pl.CostEstimate(flops=flops, bytes_accessed=nbytes, transcendentals=0),
    )


def column_sum(ref, at, function):
    rows = ref.shape[0]
    total = jnp.zeros((8, 128), F32)
    for start in range(0, rows, 64):
        size = min(64, rows - start)
        value = function(ref[start : start + size, at].astype(F32))
        total += jnp.sum(value.reshape(size // 8, 8, value.shape[1]), axis=0)
    return jnp.sum(total, axis=0, keepdims=True)


def norm_kernel(begin, end, spans, loaded, img_ref, x_ref, mods_ref, w_ref, *refs):
    known = refs[2:4] if begin else ()
    refs = refs[len(known) + 2 :] if begin else refs
    own_ref, other_ref = refs[:2]
    load_refs, refs = refs[2 : 2 + loaded], refs[2 + loaded :]
    part_refs = refs[: len(known)]
    img_scr, sel_scr, sems, *more = refs[len(known) :]
    mine = lax.axis_index("rep")
    rows, half = own_ref.shape
    width_in = x_ref.shape[0]
    tiles = img_ref.shape[0]
    step = 128
    per_tile = rows // tiles
    steps = (end - begin) // step
    early = [pltpu.make_async_copy(img_ref, img_scr, sems.at[0])]
    x_copies = [None] * steps
    copies = []
    if not begin:
        x_scr, mods_scr = more
        early.append(pltpu.make_async_copy(mods_ref, mods_scr, sems.at[1]))
        x_copies = [
            pltpu.make_async_copy(
                x_ref.at[:, pl.ds(i * step, step)], x_scr.at[:, pl.ds(i * step, step)], sems.at[3 + i]
            )
            for i in range(steps)
        ]
        copies.append(pltpu.make_async_copy(x_ref.at[:, pl.ds(end, rows - end)], load_refs[-1], sems.at[2]))
        for copy in x_copies[:1] + early + x_copies[1:]:
            copy.start()
        x_ref, mods_ref = x_scr, mods_scr
    else:
        early[0].start()
    copies = [
        pltpu.make_async_copy(
            w_ref.at[plane, :, pl.ds(start, size)], load_refs[out].at[at, :, pl.ds(left, size)],
            sems.at[3 + steps + i],
        )
        for i, (out, plane, start, size, at, left) in enumerate(spans)
    ] + copies
    for copy in copies:
        copy.start()
    products = product_list(own_ref, known, part_refs, slice(0, begin))
    total = steps * 2 * -(-half // step)
    count, done = 0, 0
    for index in range(steps):
        start = begin + index * step
        at = slice(start, start + step)
        t = start // per_tile
        x_at = slice(index * step, (index + 1) * step)
        if x_copies[index] is not None:
            x_copies[index].wait()
        mean = column_sum(x_ref, x_at, lambda v: v) / width_in
        var = column_sum(x_ref, x_at, lambda v: (v - mean) ** 2) / width_in
        inv = 1.0 / jnp.sqrt(var + 1e-06)
        mean = jnp.broadcast_to(mean, (step, step)).T
        inv = jnp.broadcast_to(inv, (step, step)).T
        if not index:
            for copy in early:
                copy.wait()
        if not index or start % per_tile == 0:
            mods = mods_ref[img_scr[t]]
            for row in range(2):
                low, high = mods[row : row + 1, :half], mods[row : row + 1, half:]
                if row:
                    low, high = 1.0 + low, 1.0 + high
                sel_scr[t, row : row + 1] = jnp.where(mine == 0, low, high)
                sel_scr[t, 2 + row : 3 + row] = jnp.where(mine == 0, high, low)
        for which, out in enumerate((own_ref, other_ref)):
            base = (mine if which == 0 else 1 - mine) * half
            for left in range(0, half, step):
                size = min(step, half - left)
                first = pl.multiple_of(base + left, 16)
                value = x_ref[pl.ds(first, size), x_at].T.astype(F32)
                lanes = slice(left, left + size)
                shift = sel_scr[t, 2 * which : 2 * which + 1, lanes]
                scale = sel_scr[t, 2 * which + 1 : 2 * which + 2, lanes]
                out[at, lanes] = (
                    (value - mean[:, :size]) * inv[:, :size] * scale + shift
                ).astype(BF16)
                count += 1
                while done * total < count * len(products):
                    products[done]()
                    done += 1
    for copy in copies:
        copy.wait()


def product_list(own_ref, w_refs, part_refs, rows):
    def product(w_ref, part_ref, c, lanes):
        part_ref[c, rows, lanes] = jnp.dot(
            own_ref[rows, :], w_ref[c, :, lanes], preferred_element_type=F32
        )

    return [
        functools.partial(product, w_ref, part_ref, c, slice(at, min(at + 256, w_ref.shape[2])))
        for w_ref, part_ref in zip(w_refs, part_refs)
        for c in range(w_ref.shape[0])
        for at in range(0, w_ref.shape[2], 256)
    ]


def query_kernel(own_ref, other_ref, w_ref, w_other_ref, q_ref):
    total = jnp.dot(own_ref[...], w_ref[...], preferred_element_type=F32)
    total += jnp.dot(other_ref[...], w_other_ref[...], preferred_element_type=F32)
    q_ref[...] = jnp.maximum(total, 0.0).astype(BF16)


def part_kernel(begin, own_ref, w0_ref, w1_ref, after_ref, *refs):
    outs = refs[-2:]
    for product in product_list(own_ref, (w0_ref, w1_ref), outs, slice(begin, own_ref.shape[0])):
        product()


def head_blocks(width):
    return [(start, min(128, width - start)) for start in range(0, width, 128)]


def same_head(rows, cols):
    return (
        lax.broadcasted_iota(jnp.int32, (rows, cols), 0) // HD
        == lax.broadcasted_iota(jnp.int32, (rows, cols), 1) // HD
    )


def state_rows(tiles):
    return tiles * HD + 8


def second_kernel(offset, img_ref, mod_ref, w_ref, part_ref, *refs):
    state_ref, k_scr, v_scr, img_scr, sem = refs[-5:]
    rows, width = k_scr.shape
    tiles = img_ref.shape[0]
    per_tile = rows // tiles
    img_copy = pltpu.make_async_copy(img_ref, img_scr, sem)
    img_copy.start()
    mod = mod_ref[...]
    for c in range(w_ref.shape[0]):
        total = part_ref[c] + jnp.dot(mod, w_ref[c], preferred_element_type=F32)
        if c == 0:
            k_scr[...] = jnp.maximum(total[:, :width], 0.0).astype(BF16)
        if c == w_ref.shape[0] - 1:
            v_scr[...] = total[:, total.shape[1] - width :].astype(BF16)
    img_copy.wait()
    sums, images = [], []
    for t in range(tiles):
        span = slice(t * per_tile, (t + 1) * per_tile)
        sums.append(jnp.sum(k_scr[span, :].astype(F32), axis=0, keepdims=True))
        images.append(jnp.full((1, width), img_scr[t].astype(F32), F32))
        for start, size in head_blocks(width):
            full = lax.dot_general(
                v_scr[span, start : start + size],
                k_scr[span, start : start + size],
                (((0,), (0,)), ((), ())),
                preferred_element_type=F32,
            )
            full = jnp.where(same_head(size, size), full, 0.0)
            state_ref[t * HD : (t + 1) * HD, offset + start : offset + start + size] = sum(
                full[j * HD : (j + 1) * HD, :] for j in range(size // HD)
            ).astype(BF16)
    state_ref[tiles * HD :, offset : offset + width] = tail_rows(sums, images).astype(BF16)


def tail_rows(sums, images):
    rest = [s - s.astype(BF16).astype(F32) for s in sums]
    rows = sums + rest + images
    rows.append(jnp.zeros((8 - len(rows), sums[0].shape[1]), F32))
    return jnp.concatenate(rows, axis=0)


def add_states(totals, sums, want, blocks, tiles):
    for ref in blocks:
        tail = ref[tiles * HD :, :].astype(F32)
        for s in range(tiles):
            state = ref[s * HD : (s + 1) * HD, :].astype(F32)
            ksum = tail[s : s + 1] + tail[tiles + s : tiles + s + 1]
            for t in range(tiles):
                keep = (tail[2 * tiles + s : 2 * tiles + s + 1] == want[t : t + 1]).astype(F32)
                totals[t] += keep * state
                sums[t] += keep * ksum


def wanted(ref, tiles):
    return ref[tiles * HD :, :].astype(F32)[2 * tiles : 3 * tiles]


def sum_kernel(*refs):
    blocks, wide_ref = refs[:-1], refs[-1]
    width = wide_ref.shape[1]
    tiles = (wide_ref.shape[0] - 8) // HD
    totals = [jnp.zeros((HD, width), F32)] * tiles
    sums = [jnp.zeros((1, width), F32)] * tiles
    add_states(totals, sums, wanted(blocks[0], tiles), blocks, tiles)
    for t in range(tiles):
        wide_ref[t * HD : (t + 1) * HD, :] = totals[t]
    wide_ref[tiles * HD :, :] = jnp.concatenate(
        sums + [jnp.zeros((8 - tiles, width), F32)], axis=0
    )


def last_kernel(own_ref, so_far_ref, block_ref, wide_ref, out_ref):
    tiles = (out_ref.shape[0] - 8) // HD
    totals = [so_far_ref[t * HD : (t + 1) * HD, :] for t in range(tiles)]
    known = so_far_ref[tiles * HD :, :]
    sums = [known[t : t + 1] for t in range(tiles)]
    add_states(totals, sums, wanted(own_ref, tiles), (block_ref,), tiles)
    for t in range(tiles):
        wide_ref[t * HD : (t + 1) * HD, :] = totals[t]
        out_ref[t * HD : (t + 1) * HD, :] = totals[t].astype(BF16)
    tail = tail_rows(sums, [])
    wide_ref[tiles * HD :, :] = tail
    out_ref[tiles * HD :, :] = tail.astype(BF16)


def attend(q_refs, state_ref, out_ref, tiles):
    width, rows = out_ref.shape
    per_tile = rows // tiles
    first = q_refs[0].shape[1]
    exact = state_ref.dtype == F32
    tail = state_ref[tiles * HD :, :].astype(F32)
    for t in range(tiles):
        span = slice(t * per_tile, (t + 1) * per_tile)
        for start, size in head_blocks(width):
            lanes = slice(start, start + size)
            mask = same_head(size, size)
            state = state_ref[t * HD : (t + 1) * HD, lanes].astype(F32)
            state = jnp.concatenate([state] * (size // HD), axis=0)
            heads = size // HD
            parts = [jnp.where(mask, state, 0.0)]
            if exact:
                parts.append(parts[0] - parts[0].astype(BF16).astype(F32))
            row = lax.broadcasted_iota(jnp.int32, (8, size), 0)
            head = lax.broadcasted_iota(jnp.int32, (8, size), 1) // HD
            sums = jnp.where(row < 4, tail[t : t + 1, lanes], tail[tiles + t : tiles + t + 1, lanes])
            parts.append(jnp.where(row % 4 == head, sums, 0.0))
            left = jnp.concatenate(parts, axis=0).astype(BF16)
            both = lax.dot_general(
                left,
                q_refs[0][span, lanes] if start < first else q_refs[1][span, start - first : start - first + size],
                (((1,), (1,)), ((), ())), preferred_element_type=F32,
            )
            numer = both[:size]
            if exact:
                numer += both[size : 2 * size]
            sums = both[-8:]
            inverse = 1.0 / (sums[:4] + sums[4:] + 1e-06)
            inverse = jnp.concatenate(
                [jnp.broadcast_to(inverse[j : j + 1], (HD, per_tile)) for j in range(heads)], axis=0
            )
            out_ref[start : start + size, span] = (numer * inverse).astype(BF16)


def fetch_weights(p, width, w_refs, w_scr, sem):
    mine = lax.axis_index("rep")
    subs = w_refs[0].shape[1] // width
    for source, ref in enumerate(w_refs):
        @pl.when((p // subs == mine) == (source == 0))
        def _():
            pltpu.make_async_copy(ref, w_scr, sem).start()

    def finish():
        pltpu.make_async_copy(w_refs[0], w_scr, sem).wait()
        weights = w_scr[...]
        chosen = weights[:, :width]
        for s in range(1, subs):
            chosen = jnp.where(p % subs == s, weights[:, s * width : (s + 1) * width], chosen)
        return chosen

    return finish


def fifth_kernel(
    img_ref, qa_ref, qb_ref, state_ref, w0_ref, w1_ref, x_ref, mods_ref, base_ref, gate_ref,
    attn_scr, w_scr, x_scr, gates_scr, img_scr, sems,
):
    m = lax.axis_index("mp")
    cols, rows = base_ref.shape
    tiles = img_ref.shape[0]
    per_tile = rows // tiles
    finish = fetch_weights(m, attn_scr.shape[0], (w0_ref, w1_ref), w_scr, sems.at[0])
    copies = [
        pltpu.make_async_copy(img_ref, img_scr, sems.at[1]),
        pltpu.make_async_copy(x_ref.at[pl.ds(m * cols, cols), :], x_scr, sems.at[2]),
        pltpu.make_async_copy(mods_ref, gates_scr, sems.at[3]),
    ]
    for copy in copies:
        copy.start()
    attend((qa_ref, qb_ref), state_ref, attn_scr, tiles)
    weights = finish()
    for copy in copies:
        copy.wait()
    total = jnp.dot(weights, attn_scr[...], preferred_element_type=F32)
    for t in range(tiles):
        gates = gates_scr[img_scr[t]][2:3]
        gate = gates[:, :cols]
        for p in range(1, gates.shape[1] // cols):
            gate = jnp.where(m == p, gates[:, p * cols : (p + 1) * cols], gate)
        for start in range(0, cols, 128):
            size = min(128, cols - start)
            column = jnp.broadcast_to(gate[:, start : start + size], (128, size)).T
            gate_ref[start : start + size, t * 128 : (t + 1) * 128] = column
            for left in range(t * per_tile, (t + 1) * per_tile, 128):
                piece = (slice(start, start + size), slice(left, left + 128))
                base_ref[piece] = x_scr[piece].astype(F32) + column * total[piece]


def sixth_kernel(others, mp, tiles, *refs):
    qa_refs, qb_refs, state_refs = (refs[i * others : (i + 1) * others] for i in range(3))
    w0_ref, w1_ref, base_ref, gate_ref, out_ref, attn_scr, out_scr, sems = refs[3 * others :]
    m, mine = lax.axis_index("mp"), lax.axis_index("rep")
    cols, rows = out_ref.shape
    per_tile = rows // tiles
    width = attn_scr.shape[0]
    subs = w0_ref.shape[1] // width
    for index in range(others):
        attend((qa_refs[index], qb_refs[index]), state_refs[index], attn_scr, tiles)
        p = lax.rem(m + mp - 1 - index, mp)
        last = index == others - 1
        for source, ref in enumerate((w0_ref, w1_ref)):
            for s in range(subs):
                here = jnp.logical_and((p // subs == mine) == (source == 0), p % subs == s)

                @pl.when(here)
                def _(ref=ref, s=s, last=last):
                    for number, (start, size) in enumerate(pieces(cols)):
                        span = slice(start, start + size)
                        part = jnp.dot(
                            ref[span, s * width : (s + 1) * width], attn_scr[...],
                            preferred_element_type=F32,
                        )
                        for t in range(tiles):
                            column = gate_ref[span, t * 128 : (t + 1) * 128]
                            for left in range(t * per_tile, (t + 1) * per_tile, 128):
                                lanes = slice(left, left + 128)
                                value = base_ref[span, lanes] + column * part[:, lanes]
                                if last:
                                    out_scr[span, lanes] = value.astype(BF16)
                                else:
                                    base_ref[span, lanes] = value
                        if last:
                            pltpu.make_async_copy(
                                out_scr.at[span], out_ref.at[span], sems.at[number]
                            ).start()
    for number, (start, size) in enumerate(pieces(cols)):
        span = slice(start, start + size)
        pltpu.make_async_copy(out_scr.at[span], out_ref.at[span], sems.at[number]).wait()


def pieces(cols):
    unit = cols // 16 // 4 * 16
    return [(0, cols - 2 * unit), (cols - 2 * unit, unit), (cols - unit, unit)]


def seq_order(seq):
    return [*range((seq + 1) // 2, seq), *range(1, (seq + 1) // 2)]


def body(tokens, slot_image, modulation, w_qkv, w_out, *, seq, mp):
    rows, depth = tokens.shape
    tiles = slot_image.shape[0]
    half, _, width = w_qkv.shape
    heads_half, cols = w_out.shape
    swap = [(0, 1), (1, 0)]
    in_hbm = functools.partial(pltpu.with_memory_space_constraint, memory_space=pltpu.HBM)
    shape = jax.ShapeDtypeStruct
    x = in_hbm(tokens.T)
    w = in_hbm(jnp.transpose(w_qkv, (1, 0, 2)))
    wo = w_out.T
    dma = pltpu.SemaphoreType.DMA

    def shift(value, axis, size, by):
        return lax.ppermute(value, axis, [(i, (i + by) % size) for i in range(size)])

    def swap_seq(value, d):
        if seq & (seq - 1):
            return shift(value, "seq", seq, d)
        return lax.ppermute(value, "seq", [(i, i ^ d) for i in range(seq)])

    def across(value):
        return lax.ppermute(value, "rep", swap)

    lead = min(384, -(-width // 256) * 128)
    cuts = [(0, lead), (lead, width - lead)]
    kv_shapes, kv_spans = [], []
    for out, (start, size) in enumerate(cuts):
        joined = size % 128 == 0
        kv_shapes.append((1, half, 2 * size) if joined else (2, half, size))
        for c in range(2):
            kv_spans.append((out, 1 + c, start, size, 0 if joined else c, c * size if joined else 0))
    part_shapes = [shape((a, rows, c), F32) for a, _, c in kv_shapes]

    def norm(begin, end, inputs, spans, loaded, before=(), known=()):
        spaces = [HB, VM, VM, HB] if begin else [HB] * 4
        scratch = [
            pltpu.SMEM((tiles,), jnp.int32), pltpu.VMEM((tiles, 8, half), F32),
            dma((3 + (end - begin) // 128 + len(spans),)),
        ]
        if not begin:
            scratch += [pltpu.VMEM((depth, end), BF16), pltpu.VMEM(modulation.shape, F32)]
        return call(
            functools.partial(norm_kernel, begin, end, spans, len(loaded)),
            [shape((rows, half), BF16)] * 2 + [shape(l, BF16) for l in loaded]
            + (part_shapes if known else []),
            spaces + [VM] * (len(before) + len(known)), scratch=scratch,
            aliases={4 + i: i for i in range(len(before))}, nbytes=4 * MIB,
        )(*inputs, w, *before, *known)

    split = rows // 256 * 128
    own, other, wa, *kv, x_last = norm(
        0, split, (in_hbm(slot_image), x, in_hbm(modulation)),
        [(0, 0, 0, lead, 0, 0)] + [(1 + out, *rest) for out, *rest in kv_spans],
        [(1, half, lead)] + kv_shapes + [(depth, rows - split)],
    )
    wa_theirs = across(wa)
    kv_theirs = [across(k) for k in kv]
    own, other, wb, *part = norm(
        split, rows, (slot_image, x_last, modulation), [(0, 0, lead, width - lead, 0, 0)],
        [(1, half, width - lead)], (own, other), kv,
    )
    wb_theirs = across(wb)

    def query(size, mine, theirs):
        return call(
            query_kernel, shape((rows, size), BF16), [VM] * 4,
            flops=2 * rows * depth * size, nbytes=3 * MIB,
        )(own, other, mine, theirs)

    qa = query(lead, wa[0], wa_theirs[0])
    qa_theirs = [shift(qa, "mp", mp, d) for d in range(1, mp)]
    part = call(
        functools.partial(part_kernel, split), part_shapes, [VM] * 6,
        aliases={4: 0, 5: 1}, flops=2 * rows * half * width, nbytes=4 * MIB,
    )(own, *kv, qa, *part)
    block = (state_rows(tiles), width)
    state = ()
    for i, (start, size) in enumerate(cuts):
        state = (call(
            functools.partial(second_kernel, start), shape(block, BF16),
            [HB] + [VM] * (3 + len(state)), aliases={4: 0} if state else None,
            scratch=[pltpu.VMEM((rows, size), BF16)] * 2 + [pltpu.SMEM((tiles,), jnp.int32), dma],
            flops=2 * rows * half * 2 * size, nbytes=6 * MIB,
        )(slot_image, other, kv_theirs[i], part[i], *state),)
    state = state[0]
    near = [state] + [swap_seq(state, d) for d in seq_order(seq)]
    qb = query(width - lead, wb[0], wb_theirs[0])
    qb_theirs = [shift(qb, "mp", mp, d) for d in range(1, mp)]
    wo_theirs = across(wo)
    far = [across(b) for b in near]
    so_far = call(sum_kernel, shape(block, F32), [VM] * (2 * seq - 1), nbytes=MIB)(*near, *far[:-1])
    wide, final = call(
        last_kernel, [shape(block, F32), shape(block, BF16)], [VM] * 3, nbytes=MIB
    )(near[0], so_far, far[-1])
    finals = [shift(final, "mp", mp, d) for d in range(1, mp)]
    base, gate = call(
        fifth_kernel, [shape((cols, rows), F32), shape((cols, tiles * 128), F32)],
        [HB, VM, VM, VM, HB, HB, HB, HB],
        scratch=[
            pltpu.VMEM((width, rows), BF16), pltpu.VMEM((cols, heads_half), BF16), pltpu.VMEM((cols, rows), BF16),
            pltpu.VMEM(modulation.shape, F32), pltpu.SMEM((tiles,), jnp.int32), dma((4,)),
        ],
        flops=2 * rows * width * cols, nbytes=4 * MIB,
    )(slot_image, qa, qb, wide, wo, wo_theirs, x, modulation)
    out = call(
        functools.partial(sixth_kernel, mp - 1, mp, tiles), shape((cols, rows), BF16),
        [VM] * (3 * (mp - 1) + 4), out_specs=HB,
        scratch=[pltpu.VMEM((width, rows), BF16), pltpu.VMEM((cols, rows), BF16), dma((3,))],
        flops=2 * rows * width * cols, nbytes=4 * MIB,
    )(*qa_theirs, *qb_theirs, *finals, wo, wo_theirs, base, gate)
    return out.T


def solution(mesh):
    sizes = dict(mesh.shape)

    def step(*args):
        return body(*args, seq=sizes["seq"], mp=sizes["mp"])

    return jax.shard_map(
        step,
        mesh=mesh,
        in_specs=(
            P(("groups", "seq", "rep"), None),
            P(("groups", "seq", "rep")),
            P("groups", None, None),
            P("rep", None, "mp"),
            P("rep", "mp"),
        ),
        out_specs=P(("groups", "seq", "rep"), "mp"),
        check_vma=False,
    )
```

profile of v0, /device:TPU:0, one launch (start us, length us, event | category | flops | bytes accessed | tf_op | source)
XLA Modules:
  0.0 40.9 jit_solution(2007555525371239496)
XLA Ops:
  0.0 3.1 %shard_map.55 = (bf16[512,1120]{1,0:T(8,128)(2,1)S(1)}, bf16[512,1120]{1,0:T(8,128)(2,1)S(1)}, bf16[1,1120,384]{2,1,0:T(8,128)(2,1)S(1)}, bf16[1,1120,768]{2,1,0...) custom-call(s32[2]{0:T(128)} %img_ref.9, bf16[2240,512]{1,0:T(8,128)(2,1)} %bitcast.17, ...), custom_call_target="tpu_custom_call" | custom-call | bytes 4194304 | tf_op jit(solution)/shard_map/pallas_call | solution.py:441
  3.1 0.6 %collective-permute-start.5 = (bf16[1,1120,768]{2,1,0:T(8,128)(2,1)S(1)}, bf16[1,1120,768]{2,1,0:T(8,128)(2,1)S(1)}, u32[]{:S(2)}, u32[]{:S(2)}) collective-permute-start(bf16[1,1120,768]{2,1,0:T(8,128)(2,1)S(1)} %get-tuple-element.25.refs_2_.w0_ref), channel_id=1, source_target_pairs={{0,1},{1,0},{2,3},{3,2},{4,5},{5,4},{6,7},{7,6},{8,9},{9,8},{10,11... | collective-permute-start | bytes 5160968 | tf_op jit(solution)/shard_map/ppermute | solution.py:421
  3.7 0.4 %collective-permute-start = (bf16[1,1120,384]{2,1,0:T(8,128)(2,1)S(1)}, bf16[1,1120,384]{2,1,0:T(8,128)(2,1)S(1)}, u32[]{:S(2)}, u32[]{:S(2)}) collective-permute-start(bf16[1,1120,384]{2,1,0:T(8,128)(2,1)S(1)} %get-tuple-element.29), channel_id=1, source_target_pairs={{0,1},{1,0},{2,3},{3,2},{4,5},{5,4},{6,7},{7,6},{8,9},{9,8},{10,11... | collective-permute-start | bytes 2580488 | tf_op jit(solution)/shard_map/ppermute | solution.py:421
  4.2 1.9 %shard_map.56 = (bf16[512,1120]{1,0:T(8,128)(2,1)S(1)}, bf16[512,1120]{1,0:T(8,128)(2,1)S(1)}, bf16[1,1120,256]{2,1,0:T(8,128)(2,1)S(1)}, f32[1,512,768]{2,1,0:T(8,128)S(1)}, f32[1,512,512]{2,1,0:T(8,128)S(1)}) custom-call(s32[2]{0:T(128)S(1)} %copy-done.2, ...), custom_call_target="tpu_custom_call", output_to_operand_aliasing={{0}: (4, {}), {1}: (5, {})} | custom-call | bytes 4194304 | tf_op jit(solution)/shard_map/pallas_call | solution.py:441
  6.2 0.5 %collective-permute-start.2 = (bf16[1,1120,256]{2,1,0:T(8,128)(2,1)S(1)}, bf16[1,1120,256]{2,1,0:T(8,128)(2,1)S(1)}, u32[]{:S(2)}, u32[]{:S(2)}) collective-permute-start(bf16[1,1120,256]{2,1,0:T(8,128)(2,1)S(1)} %get-tuple-element.30), channel_id=1, source_target_pairs={{0,1},{1,0},{2,3},{3,2},{4,5},{5,4},{6,7},{7,6},{8,9},{9,8},{10,11... | collective-permute-start | bytes 1720328 | tf_op jit(solution)/shard_map/ppermute | solution.py:421
  6.7 3.1 %collective-permute-done = bf16[1,1120,384]{2,1,0:T(8,128)(2,1)S(1)} collective-permute-done((bf16[1,1120,384]{2,1,0:T(8,128)(2,1)S(1)}, bf16[1,1120,384]{2,1,0:T(8,128)(2,1)S(1)}, u32[]{:S(2)}, u32[]{:S(2)}) %collective-permute-start) | collective-permute-done | bytes 860192 | tf_op jit(solution)/shard_map/ppermute | solution.py:421
  9.7 1.5 %shard_map.57.after_ref.qa_ref = bf16[512,384]{1,0:T(8,128)(2,1)S(1)} custom-call(bf16[512,1120]{1,0:T(8,128)(2,1)S(1)} %get-tuple-element.27.own_ref, bf16[512,1120]{1,0:T(8,128)(2,1)S(1)} %get-tuple-element.28.other_ref.mod_ref, bf16[1120,384]{1,0:T(8,128)(2,1)S(1)} %bitcast.11, bf16[1120,384]{1,0:T(8,128)(2,1)S(1)} %bitcast.12), custom_call_target="tpu_custom_call" | custom-call | flops 880803840 | bytes 3145728 | tf_op jit(solution)/shard_map/pallas_call | solution.py:464
  11.2 1.0 %shard_map.59 = (f32[1,512,768]{2,1,0:T(8,128)S(1)}, f32[1,512,512]{2,1,0:T(8,128)S(1)}) custom-call(bf16[512,1120]{1,0:T(8,128)(2,1)S(1)} %get-tuple-element.27.own_ref, bf16[1,1120,768]{2,1,0:T(8,128)(2,1)S(1)} %get-tuple-element.25.refs_2_.w0_ref, ...), custom_call_target="tpu_custom_call", output_to_operand_aliasing={{0}: (4, {}), {1}: (5, {})} | custom-call | flops 734003200 | bytes 4194304 | tf_op jit(solution)/shard_map/pallas_call | solution.py:471
  12.2 1.7 %shard_map.60.refs_0_ = bf16[72,640]{1,0:T(8,128)(2,1)S(1)} custom-call(s32[2]{0:T(128)S(1)} %copy-done.2, bf16[512,1120]{1,0:T(8,128)(2,1)S(1)} %get-tuple-element.28.other_ref.mod_ref, bf16[1,1120,768]{2,1,0:T(8,128)(2,1)S(1)} %collective-permute-done.5.w_ref, f32[1,512,768]{2,1,0:T(8,128)S(1)} %get-tuple-element.34.part_ref), custom_call_target="tpu_custom_call" | custom-call | flops 880803840 | bytes 6291456 | tf_op jit(solution)/shard_map/pallas_call | solution.py:478
  14.0 1.1 %shard_map.61.refs_0_.own_ref = bf16[72,640]{1,0:T(8,128)(2,1)S(1)} custom-call(s32[2]{0:T(128)S(1)} %copy-done.2, bf16[512,1120]{1,0:T(8,128)(2,1)S(1)} %get-tuple-element.28.other_ref.mod_ref, bf16[1,1120,512]{2,1,0:T(8,128)(2,1)S(1)} %collective-permute-done.4.w_ref, ...), custom_call_target="tpu_custom_call", output_to_operand_aliasing={{}: (4, {})} | custom-call | flops 587202560 | bytes 6291456 | tf_op jit(solution)/shard_map/pallas_call | solution.py:478
  15.1 4.0 %collective-permute-start.6 = (bf16[72,640]{1,0:T(8,128)(2,1)S(1)}, bf16[72,640]{1,0:T(8,128)(2,1)S(1)}, u32[]{:S(2)}, u32[]{:S(2)}) collective-permute-start(bf16[72,640]{1,0:T(8,128)(2,1)S(1)} %shard_map.61.refs_0_.own_ref), channel_id=1, source_target_pairs={{0,8},{4,12},{8,0},{12,4},{1,9},{5,13},{9,1},{13,5},{2,10},{6,14},... | collective-permute-start | bytes 276488 | tf_op jit(solution)/shard_map/ppermute | solution.py:418
  19.1 1.3 %collective-permute-start.7 = (bf16[72,640]{1,0:T(8,128)(2,1)S(1)}, bf16[72,640]{1,0:T(8,128)(2,1)S(1)}, u32[]{:S(2)}, u32[]{:S(2)}) collective-permute-start(bf16[72,640]{1,0:T(8,128)(2,1)S(1)} %shard_map.61.refs_0_.own_ref), channel_id=1, source_target_pairs={{0,12},{4,8},{8,4},{12,0},{1,13},{5,9},{9,5},{13,1},{2,14},{6,10},... | collective-permute-start | bytes 276488 | tf_op jit(solution)/shard_map/ppermute | solution.py:418
  20.5 1.5 %collective-permute-start.1 = (bf16[512,384]{1,0:T(8,128)(2,1)S(1)}, bf16[512,384]{1,0:T(8,128)(2,1)S(1)}, u32[]{:S(2)}, u32[]{:S(2)}) collective-permute-start(bf16[512,384]{1,0:T(8,128)(2,1)S(1)} %shard_map.57.after_ref.qa_ref), channel_id=1, source_target_pairs={{0,2},{2,0},{1,3},{3,1},{4,6},{6,4},{5,7},{7,5},{8,10},{10,8},{9,1... | collective-permute-start | bytes 1179656 | tf_op jit(solution)/shard_map/ppermute | solution.py:413
  22.2 4.4 %collective-permute-done.6.refs_1_ = bf16[72,640]{1,0:T(8,128)(2,1)S(1)} collective-permute-done((bf16[72,640]{1,0:T(8,128)(2,1)S(1)}, bf16[72,640]{1,0:T(8,128)(2,1)S(1)}, u32[]{:S(2)}, u32[]{:S(2)}) %collective-permute-start.6) | collective-permute-done | bytes 92192 | tf_op jit(solution)/shard_map/ppermute | solution.py:418
  26.6 0.5 %collective-permute-start.10 = (bf16[72,640]{1,0:T(8,128)(2,1)S(1)}, bf16[72,640]{1,0:T(8,128)(2,1)S(1)}, u32[]{:S(2)}, u32[]{:S(2)}) collective-permute-start(bf16[72,640]{1,0:T(8,128)(2,1)S(1)} %collective-permute-done.6.refs_1_), channel_id=1, source_target_pairs={{0,1},{1,0},{2,3},{3,2},{4,5},{5,4},{6,7},{7,6},{8,9},{9,8},{10,11... | collective-permute-start | bytes 276488 | tf_op jit(solution)/shard_map/ppermute | solution.py:421
  27.1 0.8 %shard_map.58.qb_ref = bf16[512,256]{1,0:T(8,128)(2,1)S(1)} custom-call(bf16[512,1120]{1,0:T(8,128)(2,1)S(1)} %get-tuple-element.27.own_ref, bf16[512,1120]{1,0:T(8,128)(2,1)S(1)} %get-tuple-element.28.other_ref.mod_ref, bf16[1120,256]{1,0:T(8,128)(2,1)S(1)} %bitcast.13, bf16[1120,256]{1,0:T(8,128)(2,1)S(1)} %bitcast.14), custom_call_target="tpu_custom_call" | custom-call | flops 587202560 | bytes 3145728 | tf_op jit(solution)/shard_map/pallas_call | solution.py:464
  28.0 1.8 %collective-permute-start.3 = (bf16[512,256]{1,0:T(8,128)(2,1)S(1)}, bf16[512,256]{1,0:T(8,128)(2,1)S(1)}, u32[]{:S(2)}, u32[]{:S(2)}) collective-permute-start(bf16[512,256]{1,0:T(8,128)(2,1)S(1)} %shard_map.58.qb_ref), channel_id=1, source_target_pairs={{0,2},{2,0},{1,3},{3,1},{4,6},{6,4},{5,7},{7,5},{8,10},{10,8},{9,1... | collective-permute-start | bytes 786440 | tf_op jit(solution)/shard_map/ppermute | solution.py:413
  29.9 0.5 %collective-permute-start.12 = (bf16[72,640]{1,0:T(8,128)(2,1)S(1)}, bf16[72,640]{1,0:T(8,128)(2,1)S(1)}, u32[]{:S(2)}, u32[]{:S(2)}) collective-permute-start(bf16[72,640]{1,0:T(8,128)(2,1)S(1)} %collective-permute-done.8.refs_3_), channel_id=1, source_target_pairs={{0,1},{1,0},{2,3},{3,2},{4,5},{5,4},{6,7},{7,6},{8,9},{9,8},{10,11... | collective-permute-start | bytes 276488 | tf_op jit(solution)/shard_map/ppermute | solution.py:421
  30.4 0.8 %collective-permute-done.11.refs_6_ = bf16[72,640]{1,0:T(8,128)(2,1)S(1)} collective-permute-done((bf16[72,640]{1,0:T(8,128)(2,1)S(1)}, bf16[72,640]{1,0:T(8,128)(2,1)S(1)}, u32[]{:S(2)}, u32[]{:S(2)}) %collective-permute-start.11) | collective-permute-done | bytes 92192 | tf_op jit(solution)/shard_map/ppermute | solution.py:421
  31.2 0.4 shard_map.62.so_far_ref
  31.9 2.6 %shard_map.64 = (f32[1120,512]{1,0:T(8,128)S(1)}, f32[1120,256]{1,0:T(8,128)S(1)}) custom-call(s32[2]{0:T(128)S(1)} %copy-done.2, bf16[512,384]{1,0:T(8,128)(2,1)S(1)} %shard_map.57.after_ref.qa_ref, bf16[512,256]{1,0:T(8,128)(2,1)S(1)} %shard_map.58.qb_ref, f32[72,640]{1,0:T(8,128)S(1)} %get-tuple-element.36.state_ref, bf16[1120,640]{1,0:T(8,128)(2,1)S(1)} %bitcast.9, ...), custom_call_target="tpu_custom_call" | custom-call | flops 734003200 | bytes 4194304 | tf_op jit(solution)/shard_map/pallas_call | solution.py:495
  34.5 2.7 %collective-permute-done.3.refs_1_ = bf16[512,256]{1,0:T(8,128)(2,1)S(1)} collective-permute-done((bf16[512,256]{1,0:T(8,128)(2,1)S(1)}, bf16[512,256]{1,0:T(8,128)(2,1)S(1)}, u32[]{:S(2)}, u32[]{:S(2)}) %collective-permute-start.3) | collective-permute-done | bytes 262176 | tf_op jit(solution)/shard_map/ppermute | solution.py:413
  37.2 1.5 %collective-permute-done.13.refs_2_ = bf16[72,640]{1,0:T(8,128)(2,1)S(1)} collective-permute-done((bf16[72,640]{1,0:T(8,128)(2,1)S(1)}, bf16[72,640]{1,0:T(8,128)(2,1)S(1)}, u32[]{:S(2)}, u32[]{:S(2)}) %collective-permute-start.13) | collective-permute-done | bytes 92192 | tf_op jit(solution)/shard_map/ppermute | solution.py:413
  38.7 2.2 %shard_map.65 = bf16[1120,512]{1,0:T(8,128)(2,1)} custom-call(bf16[512,384]{1,0:T(8,128)(2,1)S(1)} %collective-permute-done.1.refs_0_, bf16[512,256]{1,0:T(8,128)(2,1)S(1)} %collective-permute-done.3.refs_1_, bf16[72,640]{1,0:T(8,128)(2,1)S(1)} %collective-permute-done.13.refs_2_, bf16[1120,640]{1,0:T(8,128)(2,1)S(1)} %bitcast.10, ...), custom_call_target="tpu_custom_call" | custom-call | flops 734003200 | bytes 4194304 | tf_op jit(solution)/shard_map/pallas_call | solution.py:504
  (23 shorter events, 0.8 us)
Async XLA Ops:
  0.0 4.1 %copy-start = (bf16[640,1120]{0,1:T(8,128)(2,1)S(1)}, bf16[640,1120]{0,1:T(8,128)(2,1)}, u32[]{:S(2)}) copy-start(bf16[640,1120]{0,1:T(8,128)(2,1)} %param.9) | copy-start | bytes 4300804
  0.0 4.2 %copy-start.1 = (f32[6,3,2240]{2,1,0:T(4,128)S(1)}, f32[6,3,2240]{2,1,0:T(4,128)}, u32[]{:S(2)}) copy-start(f32[6,3,2240]{2,1,0:T(4,128)} %mods_ref.5) | copy-start | bytes 483844
  0.0 4.2 %copy-start.2 = (s32[2]{0:T(128)S(1)}, s32[2]{0:T(128)}, u32[]{:S(2)}) copy-start(s32[2]{0:T(128)} %img_ref.9) | copy-start | bytes 28
  3.1 9.2 %collective-permute-start.5 = (bf16[1,1120,768]{2,1,0:T(8,128)(2,1)S(1)}, bf16[1,1120,768]{2,1,0:T(8,128)(2,1)S(1)}, u32[]{:S(2)}, u32[]{:S(2)}) collective-permute-start(bf16[1,1120,768]{2,1,0:T(8,128)(2,1)S(1)} %get-tuple-element.25.refs_2_.w0_ref), channel_id=1, source_target_pairs={{0,1},{1,0},{2,3},{3,2},{4,5},{5,4},{6,7},{7,6},{8,9},{9,8},{10,11... | collective-permute-start | bytes 5160968 | tf_op jit(solution)/shard_map/ppermute | solution.py:421
  3.6 10.3 %collective-permute-start.4 = (bf16[1,1120,512]{2,1,0:T(8,128)(2,1)S(1)}, bf16[1,1120,512]{2,1,0:T(8,128)(2,1)S(1)}, u32[]{:S(2)}, u32[]{:S(2)}) collective-permute-start(bf16[1,1120,512]{2,1,0:T(8,128)(2,1)S(1)} %get-tuple-element.26.refs_3_.w1_ref), channel_id=1, source_target_pairs={{0,1},{1,0},{2,3},{3,2},{4,5},{5,4},{6,7},{7,6},{8,9},{9,8},{10,11... | collective-permute-start | bytes 3440648 | tf_op jit(solution)/shard_map/ppermute | solution.py:421
  3.7 6.0 %collective-permute-start = (bf16[1,1120,384]{2,1,0:T(8,128)(2,1)S(1)}, bf16[1,1120,384]{2,1,0:T(8,128)(2,1)S(1)}, u32[]{:S(2)}, u32[]{:S(2)}) collective-permute-start(bf16[1,1120,384]{2,1,0:T(8,128)(2,1)S(1)} %get-tuple-element.29), channel_id=1, source_target_pairs={{0,1},{1,0},{2,3},{3,2},{4,5},{5,4},{6,7},{7,6},{8,9},{9,8},{10,11... | collective-permute-start | bytes 2580488 | tf_op jit(solution)/shard_map/ppermute | solution.py:421
  4.1 27.7 %collective-permute-start.14 = (bf16[1120,640]{1,0:T(8,128)(2,1)S(1)}, bf16[1120,640]{1,0:T(8,128)(2,1)S(1)}, u32[]{:S(2)}, u32[]{:S(2)}) collective-permute-start(bf16[1120,640]{1,0:T(8,128)(2,1)S(1)} %bitcast.8), channel_id=1, source_target_pairs={{0,1},{1,0},{2,3},{3,2},{4,5},{5,4},{6,7},{7,6},{8,9},{9,8},{10,11... | collective-permute-start | bytes 4300808 | tf_op jit(solution)/shard_map/ppermute | solution.py:421
  6.2 15.8 %collective-permute-start.2 = (bf16[1,1120,256]{2,1,0:T(8,128)(2,1)S(1)}, bf16[1,1120,256]{2,1,0:T(8,128)(2,1)S(1)}, u32[]{:S(2)}, u32[]{:S(2)}) collective-permute-start(bf16[1,1120,256]{2,1,0:T(8,128)(2,1)S(1)} %get-tuple-element.30), channel_id=1, source_target_pairs={{0,1},{1,0},{2,3},{3,2},{4,5},{5,4},{6,7},{7,6},{8,9},{9,8},{10,11... | collective-permute-start | bytes 1720328 | tf_op jit(solution)/shard_map/ppermute | solution.py:421
  15.1 11.5 %collective-permute-start.6 = (bf16[72,640]{1,0:T(8,128)(2,1)S(1)}, bf16[72,640]{1,0:T(8,128)(2,1)S(1)}, u32[]{:S(2)}, u32[]{:S(2)}) collective-permute-start(bf16[72,640]{1,0:T(8,128)(2,1)S(1)} %shard_map.61.refs_0_.own_ref), channel_id=1, source_target_pairs={{0,8},{4,12},{8,0},{12,4},{1,9},{5,13},{9,1},{13,5},{2,10},{6,14},... | collective-permute-start | bytes 276488 | tf_op jit(solution)/shard_map/ppermute | solution.py:418
  19.1 7.5 %collective-permute-start.7 = (bf16[72,640]{1,0:T(8,128)(2,1)S(1)}, bf16[72,640]{1,0:T(8,128)(2,1)S(1)}, u32[]{:S(2)}, u32[]{:S(2)}) collective-permute-start(bf16[72,640]{1,0:T(8,128)(2,1)S(1)} %shard_map.61.refs_0_.own_ref), channel_id=1, source_target_pairs={{0,12},{4,8},{8,4},{12,0},{1,13},{5,9},{9,5},{13,1},{2,14},{6,10},... | collective-permute-start | bytes 276488 | tf_op jit(solution)/shard_map/ppermute | solution.py:418
  20.5 16.7 %collective-permute-start.1 = (bf16[512,384]{1,0:T(8,128)(2,1)S(1)}, bf16[512,384]{1,0:T(8,128)(2,1)S(1)}, u32[]{:S(2)}, u32[]{:S(2)}) collective-permute-start(bf16[512,384]{1,0:T(8,128)(2,1)S(1)} %shard_map.57.after_ref.qa_ref), channel_id=1, source_target_pairs={{0,2},{2,0},{1,3},{3,1},{4,6},{6,4},{5,7},{7,5},{8,10},{10,8},{9,1... | collective-permute-start | bytes 1179656 | tf_op jit(solution)/shard_map/ppermute | solution.py:413
  22.0 6.0 %collective-permute-start.8 = (bf16[72,640]{1,0:T(8,128)(2,1)S(1)}, bf16[72,640]{1,0:T(8,128)(2,1)S(1)}, u32[]{:S(2)}, u32[]{:S(2)}) collective-permute-start(bf16[72,640]{1,0:T(8,128)(2,1)S(1)} %shard_map.61.refs_0_.own_ref), channel_id=1, source_target_pairs={{0,4},{4,0},{8,12},{12,8},{1,5},{5,1},{9,13},{13,9},{2,6},{6,2},{1... | collective-permute-start | bytes 276488 | tf_op jit(solution)/shard_map/ppermute | solution.py:418
  26.6 3.3 %collective-permute-start.9 = (bf16[72,640]{1,0:T(8,128)(2,1)S(1)}, bf16[72,640]{1,0:T(8,128)(2,1)S(1)}, u32[]{:S(2)}, u32[]{:S(2)}) collective-permute-start(bf16[72,640]{1,0:T(8,128)(2,1)S(1)} %shard_map.61.refs_0_.own_ref), channel_id=1, source_target_pairs={{0,1},{1,0},{2,3},{3,2},{4,5},{5,4},{6,7},{7,6},{8,9},{9,8},{10,11... | collective-permute-start | bytes 276488 | tf_op jit(solution)/shard_map/ppermute | solution.py:421
  26.6 3.3 %collective-permute-start.10 = (bf16[72,640]{1,0:T(8,128)(2,1)S(1)}, bf16[72,640]{1,0:T(8,128)(2,1)S(1)}, u32[]{:S(2)}, u32[]{:S(2)}) collective-permute-start(bf16[72,640]{1,0:T(8,128)(2,1)S(1)} %collective-permute-done.6.refs_1_), channel_id=1, source_target_pairs={{0,1},{1,0},{2,3},{3,2},{4,5},{5,4},{6,7},{7,6},{8,9},{9,8},{10,11... | collective-permute-start | bytes 276488 | tf_op jit(solution)/shard_map/ppermute | solution.py:421
  28.0 9.2 %collective-permute-start.3 = (bf16[512,256]{1,0:T(8,128)(2,1)S(1)}, bf16[512,256]{1,0:T(8,128)(2,1)S(1)}, u32[]{:S(2)}, u32[]{:S(2)}) collective-permute-start(bf16[512,256]{1,0:T(8,128)(2,1)S(1)} %shard_map.58.qb_ref), channel_id=1, source_target_pairs={{0,2},{2,0},{1,3},{3,1},{4,6},{6,4},{5,7},{7,5},{8,10},{10,8},{9,1... | collective-permute-start | bytes 786440 | tf_op jit(solution)/shard_map/ppermute | solution.py:413
  29.9 1.3 %collective-permute-start.11 = (bf16[72,640]{1,0:T(8,128)(2,1)S(1)}, bf16[72,640]{1,0:T(8,128)(2,1)S(1)}, u32[]{:S(2)}, u32[]{:S(2)}) collective-permute-start(bf16[72,640]{1,0:T(8,128)(2,1)S(1)} %collective-permute-done.7.refs_2_), channel_id=1, source_target_pairs={{0,1},{1,0},{2,3},{3,2},{4,5},{5,4},{6,7},{7,6},{8,9},{9,8},{10,11... | collective-permute-start | bytes 276488 | tf_op jit(solution)/shard_map/ppermute | solution.py:421
  29.9 1.6 %collective-permute-start.12 = (bf16[72,640]{1,0:T(8,128)(2,1)S(1)}, bf16[72,640]{1,0:T(8,128)(2,1)S(1)}, u32[]{:S(2)}, u32[]{:S(2)}) collective-permute-start(bf16[72,640]{1,0:T(8,128)(2,1)S(1)} %collective-permute-done.8.refs_3_), channel_id=1, source_target_pairs={{0,1},{1,0},{2,3},{3,2},{4,5},{5,4},{6,7},{7,6},{8,9},{9,8},{10,11... | collective-permute-start | bytes 276488 | tf_op jit(solution)/shard_map/ppermute | solution.py:421
  31.6 7.1 %collective-permute-start.13 = (bf16[72,640]{1,0:T(8,128)(2,1)S(1)}, bf16[72,640]{1,0:T(8,128)(2,1)S(1)}, u32[]{:S(2)}, u32[]{:S(2)}) collective-permute-start(bf16[72,640]{1,0:T(8,128)(2,1)S(1)} %get-tuple-element.35), channel_id=1, source_target_pairs={{0,2},{2,0},{1,3},{3,1},{4,6},{6,4},{5,7},{7,5},{8,10},{10,8},{9,1... | collective-permute-start | bytes 276488 | tf_op jit(solution)/shard_map/ppermute | solution.py:413
where the time goes:
time: 41.1 us; the launch traced here: 40.9 us
  Pallas kernels  16.4 us (40%)
  waiting for transfers between devices  12.5 us (30%)
  starting transfers between devices  11.8 us (29%)
    ppermute x3, starting transfers between devices, swap_seq(): return lax.ppermute(value, 'seq', [(i, i ^ d) for i in range(seq)])  5.59 us
    pallas_call x2, Pallas kernels, norm(): call(functools.partial(norm_kernel, begin, end, spans, len(loaded)), [sha...  4.97 us
    ppermute x3, waiting for transfers between devices, swap_seq(): return lax.ppermute(value, 'seq', [(i, i ^ d) for i in range(seq)])  4.46 us
    ppermute x3, waiting for transfers between devices, shift(): lax.ppermute(value, axis, [(i, (i + by) % size) for i in range(size)])  4.19 us
    ppermute x9, waiting for transfers between devices, across(): return lax.ppermute(value, 'rep', swap)  3.88 us
    ppermute x3, starting transfers between devices, shift(): lax.ppermute(value, axis, [(i, (i + by) % size) for i in range(size)])  3.58 us
    pallas_call x2, Pallas kernels, body(): call(functools.partial(second_kernel, start), shape(block, BF16), [HB] +...  2.86 us
    ppermute x9, starting transfers between devices, across(): return lax.ppermute(value, 'rep', swap)  2.67 us
  transfers between devices with their start and end apart: 15, of which 6 were waited for; matrix products, arithmetic and copies ran while one was open for 0% of the time, Pallas kernels for 27%

commit v1 on v0

--- a/solution.py
+++ b/solution.py
@@ -41,12 +41,12 @@
 
 
 def norm_kernel(begin, end, spans, loaded, img_ref, x_ref, mods_ref, w_ref, *refs):
-    known = refs[2:4] if begin else ()
+    known = refs[2:3] if begin else ()
     refs = refs[len(known) + 2 :] if begin else refs
     own_ref, other_ref = refs[:2]
     load_refs, refs = refs[2 : 2 + loaded], refs[2 + loaded :]
-    part_refs = refs[: len(known)]
-    img_scr, sel_scr, sems, *more = refs[len(known) :]
+    part_refs = refs[: 2 * len(known)]
+    img_scr, sel_scr, sems, *more = refs[2 * len(known) :]
     mine = lax.axis_index("rep")
     rows, half = own_ref.shape
     width_in = x_ref.shape[0]
@@ -81,7 +81,13 @@
     ] + copies
     for copy in copies:
         copy.start()
-    products = product_list(own_ref, known, part_refs, slice(0, begin))
+    known_late = (load_refs[0],) if begin else ()
+    products = product_list(own_ref, known, part_refs[:1], slice(0, begin))
+    if begin:
+        late = product_list(own_ref, known_late, part_refs[1:], slice(0, begin))
+        pending = copies[: len(spans) - 1]
+        products += [functools.partial(run_after, pending, late[0])] + late[1:]
+        copies = copies[len(pending) :]
     total = steps * 2 * -(-half // step)
     count, done = 0, 0
     for index in range(steps):
@@ -127,6 +133,12 @@
         copy.wait()
 
 
+def run_after(copies, function):
+    for copy in copies:
+        copy.wait()
+    function()
+
+
 def product_list(own_ref, w_refs, part_refs, rows):
     def product(w_ref, part_ref, c, lanes):
         part_ref[c, rows, lanes] = jnp.dot(
@@ -225,30 +237,35 @@
     return ref[tiles * HD :, :].astype(F32)[2 * tiles : 3 * tiles]
 
 
-def sum_kernel(*refs):
-    blocks, wide_ref = refs[:-1], refs[-1]
-    width = wide_ref.shape[1]
-    tiles = (wide_ref.shape[0] - 8) // HD
-    totals = [jnp.zeros((HD, width), F32)] * tiles
-    sums = [jnp.zeros((1, width), F32)] * tiles
-    add_states(totals, sums, wanted(blocks[0], tiles), blocks, tiles)
-    for t in range(tiles):
-        wide_ref[t * HD : (t + 1) * HD, :] = totals[t]
-    wide_ref[tiles * HD :, :] = jnp.concatenate(
-        sums + [jnp.zeros((8 - tiles, width), F32)], axis=0
-    )
-
-
-def last_kernel(own_ref, so_far_ref, block_ref, wide_ref, out_ref):
+def sum_kernel(known, *refs):
+    own_ref, their_ref, before, blocks = refs[0], refs[1], refs[2 : 2 + known], refs[2 + known : -2]
+    outs = refs[-2:]
+    width = own_ref.shape[1]
+    tiles = (own_ref.shape[0] - 8) // HD
+    for side, (ref, out) in enumerate(zip((own_ref, their_ref), outs)):
+        if known:
+            totals = [before[side][t * HD : (t + 1) * HD, :] for t in range(tiles)]
+            tail = before[side][tiles * HD :, :]
+            sums = [tail[t : t + 1] for t in range(tiles)]
+        else:
+            totals = [jnp.zeros((HD, width), F32)] * tiles
+            sums = [jnp.zeros((1, width), F32)] * tiles
+        add_states(totals, sums, wanted(ref, tiles), blocks, tiles)
+        for t in range(tiles):
+            out[t * HD : (t + 1) * HD, :] = totals[t]
+        out[tiles * HD :, :] = jnp.concatenate(
+            sums + [jnp.zeros((8 - tiles, width), F32)], axis=0
+        )
+
+
+def last_kernel(mine_ref, theirs_ref, wide_ref, out_ref):
     tiles = (out_ref.shape[0] - 8) // HD
-    totals = [so_far_ref[t * HD : (t + 1) * HD, :] for t in range(tiles)]
-    known = so_far_ref[tiles * HD :, :]
-    sums = [known[t : t + 1] for t in range(tiles)]
-    add_states(totals, sums, wanted(own_ref, tiles), (block_ref,), tiles)
-    for t in range(tiles):
-        wide_ref[t * HD : (t + 1) * HD, :] = totals[t]
-        out_ref[t * HD : (t + 1) * HD, :] = totals[t].astype(BF16)
-    tail = tail_rows(sums, [])
+    states = slice(0, tiles * HD)
+    total = mine_ref[states, :] + theirs_ref[states, :]
+    wide_ref[states, :] = total
+    out_ref[states, :] = total.astype(BF16)
+    tail = mine_ref[tiles * HD :, :] + theirs_ref[tiles * HD :, :]
+    tail = tail_rows([tail[t : t + 1] for t in range(tiles)], [])
     wide_ref[tiles * HD :, :] = tail
     out_ref[tiles * HD :, :] = tail.astype(BF16)
 
@@ -447,17 +464,20 @@
         )(*inputs, w, *before, *known)
 
     split = rows // 256 * 128
-    own, other, wa, *kv, x_last = norm(
+    own, other, wa, kv_0, x_last = norm(
         0, split, (in_hbm(slot_image), x, in_hbm(modulation)),
-        [(0, 0, 0, lead, 0, 0)] + [(1 + out, *rest) for out, *rest in kv_spans],
-        [(1, half, lead)] + kv_shapes + [(depth, rows - split)],
+        [(0, 0, 0, lead, 0, 0)] + [(1, *rest) for out, *rest in kv_spans if out == 0],
+        [(1, half, lead), kv_shapes[0], (depth, rows - split)],
     )
     wa_theirs = across(wa)
-    kv_theirs = [across(k) for k in kv]
-    own, other, wb, *part = norm(
-        split, rows, (slot_image, x_last, modulation), [(0, 0, lead, width - lead, 0, 0)],
-        [(1, half, width - lead)], (own, other), kv,
+    kv_theirs = [across(kv_0)]
+    own, other, kv_1, wb, *part = norm(
+        split, rows, (slot_image, x_last, modulation),
+        [(0, *rest) for out, *rest in kv_spans if out == 1] + [(1, 0, lead, width - lead, 0, 0)],
+        [kv_shapes[1], (1, half, width - lead)], (own, other), (kv_0,),
     )
+    kv = [kv_0, kv_1]
+    kv_theirs.append(across(kv_1))
     wb_theirs = across(wb)
 
     def query(size, mine, theirs):
@@ -486,11 +506,17 @@
     qb = query(width - lead, wb[0], wb_theirs[0])
     qb_theirs = [shift(qb, "mp", mp, d) for d in range(1, mp)]
     wo_theirs = across(wo)
-    far = [across(b) for b in near]
-    so_far = call(sum_kernel, shape(block, F32), [VM] * (2 * seq - 1), nbytes=MIB)(*near, *far[:-1])
+    their_state = across(state)
+    both = [shape(block, F32)] * 2
+    begun = call(functools.partial(sum_kernel, 0), both, [VM] * 4, nbytes=MIB)(
+        state, their_state, *near[:2]
+    )
+    mine, theirs = call(
+        functools.partial(sum_kernel, 2), both, [VM] * (2 + seq), nbytes=MIB
+    )(state, their_state, *begun, *near[2:])
     wide, final = call(
-        last_kernel, [shape(block, F32), shape(block, BF16)], [VM] * 3, nbytes=MIB
-    )(near[0], so_far, far[-1])
+        last_kernel, [shape(block, F32), shape(block, BF16)], [VM] * 2, nbytes=MIB
+    )(mine, across(theirs))
     finals = [shift(final, "mp", mp, d) for d in range(1, mp)]
     base, gate = call(
         fifth_kernel, [shape((cols, rows), F32), shape((cols, tiles * 128), F32)],

time: 41.1 us -> 46 us (1.12)
  waiting for transfers between devices: 12.5 us -> 18.2 us
  starting transfers between devices: 11.8 us -> 11.3 us
    ppermute x3, waiting for transfers between devices: 4.19 us -> 9.11 us  [shift(): lax.ppermute(value, axis, [(i, (i + by) % size) for i in range(size)])]
    ppermute x3, waiting for transfers between devices: 4.46 us -> 5.92 us  [swap_seq(): return lax.ppermute(value, 'seq', [(i, i ^ d) for i in range(seq)])]
    ppermute x9 -> x7, waiting for transfers between devices: 3.88 us -> 3.14 us  [across(): return lax.ppermute(value, 'rep', swap)]
    ppermute x9 -> x7, starting transfers between devices: 2.67 us -> 2.02 us  [across(): return lax.ppermute(value, 'rep', swap)]
  transfers between devices with their start and end apart: 15 -> 13, of which waited for: 6 -> 5; matrix products, arithmetic and copies ran while one was open for 0% -> 0% of each run, Pallas kernels for 27% -> 25%
where the time goes in v1:
time: 46 us; the launch traced here: 45.8 us
  waiting for transfers between devices  18.2 us (40%)
  Pallas kernels  16.2 us (35%)
  starting transfers between devices  11.3 us (25%)
    ppermute x3, waiting for transfers between devices, shift(): lax.ppermute(value, axis, [(i, (i + by) % size) for i in range(size)])  9.11 us
    ppermute x3, waiting for transfers between devices, swap_seq(): return lax.ppermute(value, 'seq', [(i, i ^ d) for i in range(seq)])  5.92 us
    ppermute x3, starting transfers between devices, swap_seq(): return lax.ppermute(value, 'seq', [(i, i ^ d) for i in range(seq)])  5.42 us
    pallas_call x2, Pallas kernels, norm(): call(functools.partial(norm_kernel, begin, end, spans, len(loaded)), [sha...  4.73 us
    ppermute x3, starting transfers between devices, shift(): lax.ppermute(value, axis, [(i, (i + by) % size) for i in range(size)])  3.87 us
    ppermute x7, waiting for transfers between devices, across(): return lax.ppermute(value, 'rep', swap)  3.14 us
    pallas_call x2, Pallas kernels, body(): call(functools.partial(second_kernel, start), shape(block, BF16), [HB] +...  2.89 us
    pallas_call x1, Pallas kernels, body(): call(fifth_kernel, [shape((cols, rows), F32), shape((cols, tiles * 128),...  2.61 us
  transfers between devices with their start and end apart: 13, of which 5 were waited for; matrix products, arithmetic and copies ran while one was open for 0% of the time, Pallas kernels for 25%

profile of v1, /device:TPU:0, one launch (start us, length us, event | category | flops | bytes accessed | tf_op | source)
XLA Modules:
  0.0 45.8 jit_solution(7547450787958135362)
XLA Ops:
  0.0 2.6 %shard_map.55 = (bf16[512,1120]{1,0:T(8,128)(2,1)S(1)}, bf16[512,1120]{1,0:T(8,128)(2,1)S(1)}, bf16[1,1120,384]{2,1,0:T(8,128)(2,1)S(1)}, bf16[1,1120,768]{2,1,0:T(8,128)(2,1)S(1)}, bf16[2240,256]{1,0:T(8,128)(2,1)S(1)}) custom-call(s32[2]{0:T(128)} %img_ref.9, bf16[2240,512]{1,0:T(8,128)(2,1)} %bitcast.17, f32[6,3,2240]{2,1,0:T(4,128)} %mods_ref.5, ...), custom_call_target="tpu_custom_call" | custom-call | bytes 4194304 | tf_op jit(solution)/shard_map/pallas_call | solution.py:458
  2.6 0.6 %collective-permute-start.5 = (bf16[1,1120,768]{2,1,0:T(8,128)(2,1)S(1)}, bf16[1,1120,768]{2,1,0:T(8,128)(2,1)S(1)}, u32[]{:S(2)}, u32[]{:S(2)}) collective-permute-start(bf16[1,1120,768]{2,1,0:T(8,128)(2,1)S(1)} %get-tuple-element.29.refs_2_.w0_ref), channel_id=1, source_target_pairs={{0,1},{1,0},{2,3},{3,2},{4,5},{5,4},{6,7},{7,6},{8,9},{9,8},{10,11... | collective-permute-start | bytes 5160968 | tf_op jit(solution)/shard_map/ppermute | solution.py:438
  3.2 2.1 %shard_map.56 = (bf16[512,1120]{1,0:T(8,128)(2,1)S(1)}, bf16[512,1120]{1,0:T(8,128)(2,1)S(1)}, bf16[1,1120,512]{2,1,0:T(8,128)(2,1)S(1)}, bf16[1,1120,256]{2,1,0...) custom-call(s32[2]{0:T(128)S(1)} %copy-done.2, ...), custom_call_target="tpu_custom_call", output_to_operand_aliasing={{0}: (4, {}), {1}: (5, {})} | custom-call | bytes 4194304 | tf_op jit(solution)/shard_map/pallas_call | solution.py:458
  5.4 0.5 %collective-permute-start = (bf16[1,1120,384]{2,1,0:T(8,128)(2,1)S(1)}, bf16[1,1120,384]{2,1,0:T(8,128)(2,1)S(1)}, u32[]{:S(2)}, u32[]{:S(2)}) collective-permute-start(bf16[1,1120,384]{2,1,0:T(8,128)(2,1)S(1)} %get-tuple-element.32), channel_id=1, source_target_pairs={{0,1},{1,0},{2,3},{3,2},{4,5},{5,4},{6,7},{7,6},{8,9},{9,8},{10,11... | collective-permute-start | bytes 2580488 | tf_op jit(solution)/shard_map/ppermute | solution.py:438
  6.0 0.4 collective-permute-start.2
  6.4 3.0 %collective-permute-done = bf16[1,1120,384]{2,1,0:T(8,128)(2,1)S(1)} collective-permute-done((bf16[1,1120,384]{2,1,0:T(8,128)(2,1)S(1)}, bf16[1,1120,384]{2,1,0:T(8,128)(2,1)S(1)}, u32[]{:S(2)}, u32[]{:S(2)}) %collective-permute-start) | collective-permute-done | bytes 860192 | tf_op jit(solution)/shard_map/ppermute | solution.py:438
  9.4 1.5 %shard_map.57.after_ref.qa_ref = bf16[512,384]{1,0:T(8,128)(2,1)S(1)} custom-call(bf16[512,1120]{1,0:T(8,128)(2,1)S(1)} %get-tuple-element.30.own_ref, bf16[512,1120]{1,0:T(8,128)(2,1)S(1)} %get-tuple-element.31.other_ref.mod_ref, bf16[1120,384]{1,0:T(8,128)(2,1)S(1)} %bitcast.11, bf16[1120,384]{1,0:T(8,128)(2,1)S(1)} %bitcast.12), custom_call_target="tpu_custom_call" | custom-call | flops 880803840 | bytes 3145728 | tf_op jit(solution)/shard_map/pallas_call | solution.py:484
  10.9 1.0 %shard_map.59 = (f32[1,512,768]{2,1,0:T(8,128)S(1)}, f32[1,512,512]{2,1,0:T(8,128)S(1)}) custom-call(bf16[512,1120]{1,0:T(8,128)(2,1)S(1)} %get-tuple-element.30.own_ref, bf16[1,1120,768]{2,1,0:T(8,128)(2,1)S(1)} %get-tuple-element.29.refs_2_.w0_ref, ...), custom_call_target="tpu_custom_call", output_to_operand_aliasing={{0}: (4, {}), {1}: (5, {})} | custom-call | flops 734003200 | bytes 4194304 | tf_op jit(solution)/shard_map/pallas_call | solution.py:491
  11.9 1.7 %shard_map.60.refs_0_ = bf16[72,640]{1,0:T(8,128)(2,1)S(1)} custom-call(s32[2]{0:T(128)S(1)} %copy-done.2, bf16[512,1120]{1,0:T(8,128)(2,1)S(1)} %get-tuple-element.31.other_ref.mod_ref, bf16[1,1120,768]{2,1,0:T(8,128)(2,1)S(1)} %collective-permute-done.5.w_ref, f32[1,512,768]{2,1,0:T(8,128)S(1)} %get-tuple-element.38.part_ref), custom_call_target="tpu_custom_call" | custom-call | flops 880803840 | bytes 6291456 | tf_op jit(solution)/shard_map/pallas_call | solution.py:498
  13.7 1.1 %shard_map.61.refs_0_.refs_2_ = bf16[72,640]{1,0:T(8,128)(2,1)S(1)} custom-call(s32[2]{0:T(128)S(1)} %copy-done.2, bf16[512,1120]{1,0:T(8,128)(2,1)S(1)} %get-tuple-element.31.other_ref.mod_ref, bf16[1,1120,512]{2,1,0:T(8,128)(2,1)S(1)} %collective-permute-done.4.w_ref, ...), custom_call_target="tpu_custom_call", output_to_operand_aliasing={{}: (4, {})} | custom-call | flops 587202560 | bytes 6291456 | tf_op jit(solution)/shard_map/pallas_call | solution.py:498
  14.8 0.3 collective-permute-start.6
  15.1 3.8 %collective-permute-start.7 = (bf16[72,640]{1,0:T(8,128)(2,1)S(1)}, bf16[72,640]{1,0:T(8,128)(2,1)S(1)}, u32[]{:S(2)}, u32[]{:S(2)}) collective-permute-start(bf16[72,640]{1,0:T(8,128)(2,1)S(1)} %shard_map.61.refs_0_.refs_2_), channel_id=1, source_target_pairs={{0,8},{4,12},{8,0},{12,4},{1,9},{5,13},{9,1},{13,5},{2,10},{6,14},... | collective-permute-start | bytes 276488 | tf_op jit(solution)/shard_map/ppermute | solution.py:435
  19.0 1.3 %collective-permute-start.8 = (bf16[72,640]{1,0:T(8,128)(2,1)S(1)}, bf16[72,640]{1,0:T(8,128)(2,1)S(1)}, u32[]{:S(2)}, u32[]{:S(2)}) collective-permute-start(bf16[72,640]{1,0:T(8,128)(2,1)S(1)} %shard_map.61.refs_0_.refs_2_), channel_id=1, source_target_pairs={{0,12},{4,8},{8,4},{12,0},{1,13},{5,9},{9,5},{13,1},{2,14},{6,10},... | collective-permute-start | bytes 276488 | tf_op jit(solution)/shard_map/ppermute | solution.py:435
  20.3 0.2 collective-permute-start.9
  20.5 5.9 %collective-permute-done.7.refs_3_ = bf16[72,640]{1,0:T(8,128)(2,1)S(1)} collective-permute-done((bf16[72,640]{1,0:T(8,128)(2,1)S(1)}, bf16[72,640]{1,0:T(8,128)(2,1)S(1)}, u32[]{:S(2)}, u32[]{:S(2)}) %collective-permute-start.7) | collective-permute-done | bytes 92192 | tf_op jit(solution)/shard_map/ppermute | solution.py:435
  26.5 1.8 %collective-permute-start.1 = (bf16[512,384]{1,0:T(8,128)(2,1)S(1)}, bf16[512,384]{1,0:T(8,128)(2,1)S(1)}, u32[]{:S(2)}, u32[]{:S(2)}) collective-permute-start(bf16[512,384]{1,0:T(8,128)(2,1)S(1)} %shard_map.57.after_ref.qa_ref), channel_id=1, source_target_pairs={{0,2},{2,0},{1,3},{3,1},{4,6},{6,4},{5,7},{7,5},{8,10},{10,8},{9,1... | collective-permute-start | bytes 1179656 | tf_op jit(solution)/shard_map/ppermute | solution.py:430
  28.5 0.2 shard_map.63
  28.8 0.8 %shard_map.58.qb_ref = bf16[512,256]{1,0:T(8,128)(2,1)S(1)} custom-call(bf16[512,1120]{1,0:T(8,128)(2,1)S(1)} %get-tuple-element.30.own_ref, bf16[512,1120]{1,0:T(8,128)(2,1)S(1)} %get-tuple-element.31.other_ref.mod_ref, bf16[1120,256]{1,0:T(8,128)(2,1)S(1)} %bitcast.13, bf16[1120,256]{1,0:T(8,128)(2,1)S(1)} %bitcast.14), custom_call_target="tpu_custom_call" | custom-call | flops 587202560 | bytes 3145728 | tf_op jit(solution)/shard_map/pallas_call | solution.py:484
  29.6 0.4 collective-permute-start.3
  30.2 1.6 %collective-permute-start.11 = (bf16[72,640]{1,0:T(8,128)(2,1)S(1)}, bf16[72,640]{1,0:T(8,128)(2,1)S(1)}, u32[]{:S(2)}, u32[]{:S(2)}) collective-permute-start(bf16[72,640]{1,0:T(8,128)(2,1)S(1)} %get-tuple-element.43), channel_id=1, source_target_pairs={{0,2},{2,0},{1,3},{3,1},{4,6},{6,4},{5,7},{7,5},{8,10},{10,8},{9,1... | collective-permute-start | bytes 276488 | tf_op jit(solution)/shard_map/ppermute | solution.py:430
  31.9 2.6 %shard_map.65 = (f32[1120,512]{1,0:T(8,128)S(1)}, f32[1120,256]{1,0:T(8,128)S(1)}) custom-call(s32[2]{0:T(128)S(1)} %copy-done.2, bf16[512,384]{1,0:T(8,128)(2,1)S(1)} %shard_map.57.after_ref.qa_ref, bf16[512,256]{1,0:T(8,128)(2,1)S(1)} %shard_map.58.qb_ref, f32[72,640]{1,0:T(8,128)S(1)} %get-tuple-element.44.state_ref, bf16[1120,640]{1,0:T(8,128)(2,1)S(1)} %bitcast.9, ...), custom_call_target="tpu_custom_call" | custom-call | flops 734003200 | bytes 4194304 | tf_op jit(solution)/shard_map/pallas_call | solution.py:521
  34.5 8.1 %collective-permute-done.3.refs_1_ = bf16[512,256]{1,0:T(8,128)(2,1)S(1)} collective-permute-done((bf16[512,256]{1,0:T(8,128)(2,1)S(1)}, bf16[512,256]{1,0:T(8,128)(2,1)S(1)}, u32[]{:S(2)}, u32[]{:S(2)}) %collective-permute-start.3) | collective-permute-done | bytes 262176 | tf_op jit(solution)/shard_map/ppermute | solution.py:430
  42.6 1.0 %collective-permute-done.11.refs_2_ = bf16[72,640]{1,0:T(8,128)(2,1)S(1)} collective-permute-done((bf16[72,640]{1,0:T(8,128)(2,1)S(1)}, bf16[72,640]{1,0:T(8,128)(2,1)S(1)}, u32[]{:S(2)}, u32[]{:S(2)}) %collective-permute-start.11) | collective-permute-done | bytes 92192 | tf_op jit(solution)/shard_map/ppermute | solution.py:430
  43.6 2.2 %shard_map.66 = bf16[1120,512]{1,0:T(8,128)(2,1)} custom-call(bf16[512,384]{1,0:T(8,128)(2,1)S(1)} %collective-permute-done.1.refs_0_, bf16[512,256]{1,0:T(8,128)(2,1)S(1)} %collective-permute-done.3.refs_1_, bf16[72,640]{1,0:T(8,128)(2,1)S(1)} %collective-permute-done.11.refs_2_, bf16[1120,640]{1,0:T(8,128)(2,1)S(1)} %bitcast.10, ...), custom_call_target="tpu_custom_call" | custom-call | flops 734003200 | bytes 4194304 | tf_op jit(solution)/shard_map/pallas_call | solution.py:530
  (20 shorter events, 0.6 us)
Async XLA Ops:
  0.0 3.2 %copy-start.1 = (f32[6,3,2240]{2,1,0:T(4,128)S(1)}, f32[6,3,2240]{2,1,0:T(4,128)}, u32[]{:S(2)}) copy-start(f32[6,3,2240]{2,1,0:T(4,128)} %mods_ref.5) | copy-start | bytes 483844
  0.0 3.2 %copy-start.2 = (s32[2]{0:T(128)S(1)}, s32[2]{0:T(128)}, u32[]{:S(2)}) copy-start(s32[2]{0:T(128)} %img_ref.9) | copy-start | bytes 28
  2.6 9.3 %collective-permute-start.5 = (bf16[1,1120,768]{2,1,0:T(8,128)(2,1)S(1)}, bf16[1,1120,768]{2,1,0:T(8,128)(2,1)S(1)}, u32[]{:S(2)}, u32[]{:S(2)}) collective-permute-start(bf16[1,1120,768]{2,1,0:T(8,128)(2,1)S(1)} %get-tuple-element.29.refs_2_.w0_ref), channel_id=1, source_target_pairs={{0,1},{1,0},{2,3},{3,2},{4,5},{5,4},{6,7},{7,6},{8,9},{9,8},{10,11... | collective-permute-start | bytes 5160968 | tf_op jit(solution)/shard_map/ppermute | solution.py:438
  3.2 2.7 %copy-start = (bf16[640,1120]{0,1:T(8,128)(2,1)S(1)}, bf16[640,1120]{0,1:T(8,128)(2,1)}, u32[]{:S(2)}) copy-start(bf16[640,1120]{0,1:T(8,128)(2,1)} %param.9) | copy-start | bytes 4300804
  5.3 8.3 %collective-permute-start.4 = (bf16[1,1120,512]{2,1,0:T(8,128)(2,1)S(1)}, bf16[1,1120,512]{2,1,0:T(8,128)(2,1)S(1)}, u32[]{:S(2)}, u32[]{:S(2)}) collective-permute-start(bf16[1,1120,512]{2,1,0:T(8,128)(2,1)S(1)} %get-tuple-element.34.w1_ref), channel_id=1, source_target_pairs={{0,1},{1,0},{2,3},{3,2},{4,5},{5,4},{6,7},{7,6},{8,9},{9,8},{10,11... | collective-permute-start | bytes 3440648 | tf_op jit(solution)/shard_map/ppermute | solution.py:438
  5.4 4.0 %collective-permute-start = (bf16[1,1120,384]{2,1,0:T(8,128)(2,1)S(1)}, bf16[1,1120,384]{2,1,0:T(8,128)(2,1)S(1)}, u32[]{:S(2)}, u32[]{:S(2)}) collective-permute-start(bf16[1,1120,384]{2,1,0:T(8,128)(2,1)S(1)} %get-tuple-element.32), channel_id=1, source_target_pairs={{0,1},{1,0},{2,3},{3,2},{4,5},{5,4},{6,7},{7,6},{8,9},{9,8},{10,11... | collective-permute-start | bytes 2580488 | tf_op jit(solution)/shard_map/ppermute | solution.py:438
  5.9 26.0 %collective-permute-start.12 = (bf16[1120,640]{1,0:T(8,128)(2,1)S(1)}, bf16[1120,640]{1,0:T(8,128)(2,1)S(1)}, u32[]{:S(2)}, u32[]{:S(2)}) collective-permute-start(bf16[1120,640]{1,0:T(8,128)(2,1)S(1)} %bitcast.8), channel_id=1, source_target_pairs={{0,1},{1,0},{2,3},{3,2},{4,5},{5,4},{6,7},{7,6},{8,9},{9,8},{10,11... | collective-permute-start | bytes 4300808 | tf_op jit(solution)/shard_map/ppermute | solution.py:438
  6.0 22.8 %collective-permute-start.2 = (bf16[1,1120,256]{2,1,0:T(8,128)(2,1)S(1)}, bf16[1,1120,256]{2,1,0:T(8,128)(2,1)S(1)}, u32[]{:S(2)}, u32[]{:S(2)}) collective-permute-start(bf16[1,1120,256]{2,1,0:T(8,128)(2,1)S(1)} %get-tuple-element.33), channel_id=1, source_target_pairs={{0,1},{1,0},{2,3},{3,2},{4,5},{5,4},{6,7},{7,6},{8,9},{9,8},{10,11... | collective-permute-start | bytes 1720328 | tf_op jit(solution)/shard_map/ppermute | solution.py:438
  14.8 5.5 %collective-permute-start.6 = (bf16[72,640]{1,0:T(8,128)(2,1)S(1)}, bf16[72,640]{1,0:T(8,128)(2,1)S(1)}, u32[]{:S(2)}, u32[]{:S(2)}) collective-permute-start(bf16[72,640]{1,0:T(8,128)(2,1)S(1)} %shard_map.61.refs_0_.refs_2_), channel_id=1, source_target_pairs={{0,1},{1,0},{2,3},{3,2},{4,5},{5,4},{6,7},{7,6},{8,9},{9,8},{10,11... | collective-permute-start | bytes 276488 | tf_op jit(solution)/shard_map/ppermute | solution.py:438
  15.1 11.3 %collective-permute-start.7 = (bf16[72,640]{1,0:T(8,128)(2,1)S(1)}, bf16[72,640]{1,0:T(8,128)(2,1)S(1)}, u32[]{:S(2)}, u32[]{:S(2)}) collective-permute-start(bf16[72,640]{1,0:T(8,128)(2,1)S(1)} %shard_map.61.refs_0_.refs_2_), channel_id=1, source_target_pairs={{0,8},{4,12},{8,0},{12,4},{1,9},{5,13},{9,1},{13,5},{2,10},{6,14},... | collective-permute-start | bytes 276488 | tf_op jit(solution)/shard_map/ppermute | solution.py:435
  19.0 9.5 %collective-permute-start.8 = (bf16[72,640]{1,0:T(8,128)(2,1)S(1)}, bf16[72,640]{1,0:T(8,128)(2,1)S(1)}, u32[]{:S(2)}, u32[]{:S(2)}) collective-permute-start(bf16[72,640]{1,0:T(8,128)(2,1)S(1)} %shard_map.61.refs_0_.refs_2_), channel_id=1, source_target_pairs={{0,12},{4,8},{8,4},{12,0},{1,13},{5,9},{9,5},{13,1},{2,14},{6,10},... | collective-permute-start | bytes 276488 | tf_op jit(solution)/shard_map/ppermute | solution.py:435
  20.3 8.2 %collective-permute-start.9 = (bf16[72,640]{1,0:T(8,128)(2,1)S(1)}, bf16[72,640]{1,0:T(8,128)(2,1)S(1)}, u32[]{:S(2)}, u32[]{:S(2)}) collective-permute-start(bf16[72,640]{1,0:T(8,128)(2,1)S(1)} %shard_map.61.refs_0_.refs_2_), channel_id=1, source_target_pairs={{0,4},{4,0},{8,12},{12,8},{1,5},{5,1},{9,13},{13,9},{2,6},{6,2},{1... | collective-permute-start | bytes 276488 | tf_op jit(solution)/shard_map/ppermute | solution.py:435
  26.5 16.1 %collective-permute-start.1 = (bf16[512,384]{1,0:T(8,128)(2,1)S(1)}, bf16[512,384]{1,0:T(8,128)(2,1)S(1)}, u32[]{:S(2)}, u32[]{:S(2)}) collective-permute-start(bf16[512,384]{1,0:T(8,128)(2,1)S(1)} %shard_map.57.after_ref.qa_ref), channel_id=1, source_target_pairs={{0,2},{2,0},{1,3},{3,1},{4,6},{6,4},{5,7},{7,5},{8,10},{10,8},{9,1... | collective-permute-start | bytes 1179656 | tf_op jit(solution)/shard_map/ppermute | solution.py:430
  28.7 1.5 %collective-permute-start.10 = (f32[72,640]{1,0:T(8,128)S(1)}, f32[72,640]{1,0:T(8,128)S(1)}, u32[]{:S(2)}, u32[]{:S(2)}) collective-permute-start(f32[72,640]{1,0:T(8,128)S(1)} %get-tuple-element.42), channel_id=1, source_target_pairs={{0,1},{1,0},{2,3},{3,2},{4,5},{5,4},{6,7},{7,6},{8,9},{9,8},{10,11... | collective-permute-start | bytes 552968 | tf_op jit(solution)/shard_map/ppermute | solution.py:438
  29.6 12.9 %collective-permute-start.3 = (bf16[512,256]{1,0:T(8,128)(2,1)S(1)}, bf16[512,256]{1,0:T(8,128)(2,1)S(1)}, u32[]{:S(2)}, u32[]{:S(2)}) collective-permute-start(bf16[512,256]{1,0:T(8,128)(2,1)S(1)} %shard_map.58.qb_ref), channel_id=1, source_target_pairs={{0,2},{2,0},{1,3},{3,1},{4,6},{6,4},{5,7},{7,5},{8,10},{10,8},{9,1... | collective-permute-start | bytes 786440 | tf_op jit(solution)/shard_map/ppermute | solution.py:430
  30.2 13.3 %collective-permute-start.11 = (bf16[72,640]{1,0:T(8,128)(2,1)S(1)}, bf16[72,640]{1,0:T(8,128)(2,1)S(1)}, u32[]{:S(2)}, u32[]{:S(2)}) collective-permute-start(bf16[72,640]{1,0:T(8,128)(2,1)S(1)} %get-tuple-element.43), channel_id=1, source_target_pairs={{0,2},{2,0},{1,3},{3,1},{4,6},{6,4},{5,7},{7,5},{8,10},{10,8},{9,1... | collective-permute-start | bytes 276488 | tf_op jit(solution)/shard_map/ppermute | solution.py:430

commit v2 on v0

--- a/solution.py
+++ b/solution.py
@@ -41,7 +41,7 @@
 
 
 def norm_kernel(begin, end, spans, loaded, img_ref, x_ref, mods_ref, w_ref, *refs):
-    known = refs[2:4] if begin else ()
+    known = refs[2:5] if begin else ()
     refs = refs[len(known) + 2 :] if begin else refs
     own_ref, other_ref = refs[:2]
     load_refs, refs = refs[2 : 2 + loaded], refs[2 + loaded :]
@@ -141,10 +141,17 @@
     ]
 
 
-def query_kernel(own_ref, other_ref, w_ref, w_other_ref, q_ref):
-    total = jnp.dot(own_ref[...], w_ref[...], preferred_element_type=F32)
-    total += jnp.dot(other_ref[...], w_other_ref[...], preferred_element_type=F32)
-    q_ref[...] = jnp.maximum(total, 0.0).astype(BF16)
+def query_kernel(begin, own_ref, other_ref, w_ref, w_other_ref, *refs):
+    q_ref = refs[-1]
+    for first, end in ((0, begin), (begin, own_ref.shape[0])):
+        if first == end:
+            continue
+        total = jnp.dot(other_ref[first:end, :], w_other_ref[...], preferred_element_type=F32)
+        if first < begin:
+            total += refs[0][0, first:end, :]
+        else:
+            total += jnp.dot(own_ref[first:end, :], w_ref[...], preferred_element_type=F32)
+        q_ref[first:end, :] = jnp.maximum(total, 0.0).astype(BF16)
 
 
 def part_kernel(begin, own_ref, w0_ref, w1_ref, after_ref, *refs):
@@ -430,6 +437,8 @@
             kv_spans.append((out, 1 + c, start, size, 0 if joined else c, c * size if joined else 0))
     part_shapes = [shape((a, rows, c), F32) for a, _, c in kv_shapes]
 
+    split = rows // 256 * 128
+
     def norm(begin, end, inputs, spans, loaded, before=(), known=()):
         spaces = [HB, VM, VM, HB] if begin else [HB] * 4
         scratch = [
@@ -441,12 +450,11 @@
         return call(
             functools.partial(norm_kernel, begin, end, spans, len(loaded)),
             [shape((rows, half), BF16)] * 2 + [shape(l, BF16) for l in loaded]
-            + (part_shapes if known else []),
+            + ([shape((1, split, lead), F32), *part_shapes] if known else []),
             spaces + [VM] * (len(before) + len(known)), scratch=scratch,
             aliases={4 + i: i for i in range(len(before))}, nbytes=4 * MIB,
         )(*inputs, w, *before, *known)
 
-    split = rows // 256 * 128
     own, other, wa, *kv, x_last = norm(
         0, split, (in_hbm(slot_image), x, in_hbm(modulation)),
         [(0, 0, 0, lead, 0, 0)] + [(1 + out, *rest) for out, *rest in kv_spans],
@@ -454,19 +462,19 @@
     )
     wa_theirs = across(wa)
     kv_theirs = [across(k) for k in kv]
-    own, other, wb, *part = norm(
+    own, other, wb, qa_part, *part = norm(
         split, rows, (slot_image, x_last, modulation), [(0, 0, lead, width - lead, 0, 0)],
-        [(1, half, width - lead)], (own, other), kv,
+        [(1, half, width - lead)], (own, other), (wa, *kv),
     )
     wb_theirs = across(wb)
 
-    def query(size, mine, theirs):
+    def query(size, mine, theirs, begin, *known):
         return call(
-            query_kernel, shape((rows, size), BF16), [VM] * 4,
+            functools.partial(query_kernel, begin), shape((rows, size), BF16), [VM] * (4 + len(known)),
             flops=2 * rows * depth * size, nbytes=3 * MIB,
-        )(own, other, mine, theirs)
-
-    qa = query(lead, wa[0], wa_theirs[0])
+        )(own, other, mine, theirs, *known)
+
+    qa = query(lead, wa[0], wa_theirs[0], split, qa_part)
     qa_theirs = [shift(qa, "mp", mp, d) for d in range(1, mp)]
     part = call(
         functools.partial(part_kernel, split), part_shapes, [VM] * 6,
@@ -483,7 +491,7 @@
         )(slot_image, other, kv_theirs[i], part[i], *state),)
     state = state[0]
     near = [state] + [swap_seq(state, d) for d in seq_order(seq)]
-    qb = query(width - lead, wb[0], wb_theirs[0])
+    qb = query(width - lead, wb[0], wb_theirs[0], 0)
     qb_theirs = [shift(qb, "mp", mp, d) for d in range(1, mp)]
     wo_theirs = across(wo)
     far = [across(b) for b in near]

time: 41.1 us -> 40.8 us (level)
  transfers between devices with their start and end apart: 15 -> 15, of which waited for: 6 -> 6; matrix products, arithmetic and copies ran while one was open for 0% -> 0% of each run, Pallas kernels for 27% -> 28%
where the time goes in v2:
time: 40.8 us; the launch traced here: 40.6 us
  Pallas kernels  16.5 us (40%)
  waiting for transfers between devices  12.2 us (30%)
  starting transfers between devices  11.8 us (29%)
    ppermute x3, starting transfers between devices, swap_seq(): return lax.ppermute(value, 'seq', [(i, i ^ d) for i in range(seq)])  5.59 us
    pallas_call x2, Pallas kernels, norm(): call(functools.partial(norm_kernel, begin, end, spans, len(loaded)), [sha...  5.36 us
    ppermute x3, waiting for transfers between devices, swap_seq(): return lax.ppermute(value, 'seq', [(i, i ^ d) for i in range(seq)])  4.46 us
    ppermute x3, waiting for transfers between devices, shift(): lax.ppermute(value, axis, [(i, (i + by) % size) for i in range(size)])  4.21 us
    ppermute x3, starting transfers between devices, shift(): lax.ppermute(value, axis, [(i, (i + by) % size) for i in range(size)])  3.58 us
    ppermute x9, waiting for transfers between devices, across(): return lax.ppermute(value, 'rep', swap)  3.51 us
    pallas_call x2, Pallas kernels, body(): call(functools.partial(second_kernel, start), shape(block, BF16), [HB] +...  2.85 us
    ppermute x9, starting transfers between devices, across(): return lax.ppermute(value, 'rep', swap)  2.67 us
  transfers between devices with their start and end apart: 15, of which 6 were waited for; matrix products, arithmetic and copies ran while one was open for 0% of the time, Pallas kernels for 28%

profile of v2, /device:TPU:0, one launch (start us, length us, event | category | flops | bytes accessed | tf_op | source)
XLA Modules:
  0.0 40.6 jit_solution(5679719894810466323)
XLA Ops:
  0.0 3.1 %shard_map.55 = (bf16[512,1120]{1,0:T(8,128)(2,1)S(1)}, bf16[512,1120]{1,0:T(8,128)(2,1)S(1)}, bf16[1,1120,384]{2,1,0:T(8,128)(2,1)S(1)}, bf16[1,1120,768]{2,1,0...) custom-call(s32[2]{0:T(128)} %img_ref.9, bf16[2240,512]{1,0:T(8,128)(2,1)} %bitcast.17, ...), custom_call_target="tpu_custom_call" | custom-call | bytes 4194304 | tf_op jit(solution)/shard_map/pallas_call | solution.py:450
  3.1 0.6 %collective-permute-start.5 = (bf16[1,1120,768]{2,1,0:T(8,128)(2,1)S(1)}, bf16[1,1120,768]{2,1,0:T(8,128)(2,1)S(1)}, u32[]{:S(2)}, u32[]{:S(2)}) collective-permute-start(bf16[1,1120,768]{2,1,0:T(8,128)(2,1)S(1)} %get-tuple-element.27.refs_3_.w0_ref), channel_id=1, source_target_pairs={{0,1},{1,0},{2,3},{3,2},{4,5},{5,4},{6,7},{7,6},{8,9},{9,8},{10,11... | collective-permute-start | bytes 5160968 | tf_op jit(solution)/shard_map/ppermute | solution.py:428
  3.7 0.4 %collective-permute-start = (bf16[1,1120,384]{2,1,0:T(8,128)(2,1)S(1)}, bf16[1,1120,384]{2,1,0:T(8,128)(2,1)S(1)}, u32[]{:S(2)}, u32[]{:S(2)}) collective-permute-start(bf16[1,1120,384]{2,1,0:T(8,128)(2,1)S(1)} %get-tuple-element.26.refs_2_), channel_id=1, source_target_pairs={{0,1},{1,0},{2,3},{3,2},{4,5},{5,4},{6,7},{7,6},{8,9},{9,8},{10,11... | collective-permute-start | bytes 2580488 | tf_op jit(solution)/shard_map/ppermute | solution.py:428
  4.2 2.3 %shard_map.56 = (bf16[512,1120]{1,0:T(8,128)(2,1)S(1)}, bf16[512,1120]{1,0:T(8,128)(2,1)S(1)}, bf16[1,1120,256]{2,1,0:T(8,128)(2,1)S(1)}, f32[1,256,384]{2,1,0:T...) custom-call(s32[2]{0:T(128)S(1)} %copy-done.2, ...), custom_call_target="tpu_custom_call", output_to_operand_aliasing={{0}: (4, {}), {1}: (5, {})} | custom-call | bytes 4194304 | tf_op jit(solution)/shard_map/pallas_call | solution.py:450
  6.5 0.5 %collective-permute-start.2 = (bf16[1,1120,256]{2,1,0:T(8,128)(2,1)S(1)}, bf16[1,1120,256]{2,1,0:T(8,128)(2,1)S(1)}, u32[]{:S(2)}, u32[]{:S(2)}) collective-permute-start(bf16[1,1120,256]{2,1,0:T(8,128)(2,1)S(1)} %get-tuple-element.32), channel_id=1, source_target_pairs={{0,1},{1,0},{2,3},{3,2},{4,5},{5,4},{6,7},{7,6},{8,9},{9,8},{10,11... | collective-permute-start | bytes 1720328 | tf_op jit(solution)/shard_map/ppermute | solution.py:428
  7.0 2.7 %collective-permute-done = bf16[1,1120,384]{2,1,0:T(8,128)(2,1)S(1)} collective-permute-done((bf16[1,1120,384]{2,1,0:T(8,128)(2,1)S(1)}, bf16[1,1120,384]{2,1,0:T(8,128)(2,1)S(1)}, u32[]{:S(2)}, u32[]{:S(2)}) %collective-permute-start) | collective-permute-done | bytes 860192 | tf_op jit(solution)/shard_map/ppermute | solution.py:428
  9.7 1.2 %shard_map.57.after_ref.qa_ref = bf16[512,384]{1,0:T(8,128)(2,1)S(1)} custom-call(bf16[512,1120]{1,0:T(8,128)(2,1)S(1)} %get-tuple-element.29.own_ref, bf16[512,1120]{1,0:T(8,128)(2,1)S(1)} %get-tuple-element.30.other_ref.mod_ref, bf16[1120,384]{1,0:T(8,128)(2,1)S(1)} %bitcast.11, bf16[1120,384]{1,0:T(8,128)(2,1)S(1)} %bitcast.12, ...), custom_call_target="tpu_custom_call" | custom-call | flops 880803840 | bytes 3145728 | tf_op jit(solution)/shard_map/pallas_call | solution.py:472
  10.9 1.0 %shard_map.59 = (f32[1,512,768]{2,1,0:T(8,128)S(1)}, f32[1,512,512]{2,1,0:T(8,128)S(1)}) custom-call(bf16[512,1120]{1,0:T(8,128)(2,1)S(1)} %get-tuple-element.29.own_ref, bf16[1,1120,768]{2,1,0:T(8,128)(2,1)S(1)} %get-tuple-element.27.refs_3_.w0_ref, ...), custom_call_target="tpu_custom_call", output_to_operand_aliasing={{0}: (4, {}), {1}: (5, {})} | custom-call | flops 734003200 | bytes 4194304 | tf_op jit(solution)/shard_map/pallas_call | solution.py:479
  11.9 1.7 %shard_map.60.refs_0_ = bf16[72,640]{1,0:T(8,128)(2,1)S(1)} custom-call(s32[2]{0:T(128)S(1)} %copy-done.2, bf16[512,1120]{1,0:T(8,128)(2,1)S(1)} %get-tuple-element.30.other_ref.mod_ref, bf16[1,1120,768]{2,1,0:T(8,128)(2,1)S(1)} %collective-permute-done.5.w_ref, f32[1,512,768]{2,1,0:T(8,128)S(1)} %get-tuple-element.36.part_ref), custom_call_target="tpu_custom_call" | custom-call | flops 880803840 | bytes 6291456 | tf_op jit(solution)/shard_map/pallas_call | solution.py:486
  13.7 1.1 %shard_map.61.refs_0_.own_ref = bf16[72,640]{1,0:T(8,128)(2,1)S(1)} custom-call(s32[2]{0:T(128)S(1)} %copy-done.2, bf16[512,1120]{1,0:T(8,128)(2,1)S(1)} %get-tuple-element.30.other_ref.mod_ref, bf16[1,1120,512]{2,1,0:T(8,128)(2,1)S(1)} %collective-permute-done.4.w_ref, ...), custom_call_target="tpu_custom_call", output_to_operand_aliasing={{}: (4, {})} | custom-call | flops 587202560 | bytes 6291456 | tf_op jit(solution)/shard_map/pallas_call | solution.py:486
  14.8 4.0 %collective-permute-start.6 = (bf16[72,640]{1,0:T(8,128)(2,1)S(1)}, bf16[72,640]{1,0:T(8,128)(2,1)S(1)}, u32[]{:S(2)}, u32[]{:S(2)}) collective-permute-start(bf16[72,640]{1,0:T(8,128)(2,1)S(1)} %shard_map.61.refs_0_.own_ref), channel_id=1, source_target_pairs={{0,8},{4,12},{8,0},{12,4},{1,9},{5,13},{9,1},{13,5},{2,10},{6,14},... | collective-permute-start | bytes 276488 | tf_op jit(solution)/shard_map/ppermute | solution.py:425
  18.8 1.4 %collective-permute-start.7 = (bf16[72,640]{1,0:T(8,128)(2,1)S(1)}, bf16[72,640]{1,0:T(8,128)(2,1)S(1)}, u32[]{:S(2)}, u32[]{:S(2)}) collective-permute-start(bf16[72,640]{1,0:T(8,128)(2,1)S(1)} %shard_map.61.refs_0_.own_ref), channel_id=1, source_target_pairs={{0,12},{4,8},{8,4},{12,0},{1,13},{5,9},{9,5},{13,1},{2,14},{6,10},... | collective-permute-start | bytes 276488 | tf_op jit(solution)/shard_map/ppermute | solution.py:425
  20.2 1.5 %collective-permute-start.1 = (bf16[512,384]{1,0:T(8,128)(2,1)S(1)}, bf16[512,384]{1,0:T(8,128)(2,1)S(1)}, u32[]{:S(2)}, u32[]{:S(2)}) collective-permute-start(bf16[512,384]{1,0:T(8,128)(2,1)S(1)} %shard_map.57.after_ref.qa_ref), channel_id=1, source_target_pairs={{0,2},{2,0},{1,3},{3,1},{4,6},{6,4},{5,7},{7,5},{8,10},{10,8},{9,1... | collective-permute-start | bytes 1179656 | tf_op jit(solution)/shard_map/ppermute | solution.py:420
  21.9 4.4 %collective-permute-done.6.refs_1_ = bf16[72,640]{1,0:T(8,128)(2,1)S(1)} collective-permute-done((bf16[72,640]{1,0:T(8,128)(2,1)S(1)}, bf16[72,640]{1,0:T(8,128)(2,1)S(1)}, u32[]{:S(2)}, u32[]{:S(2)}) %collective-permute-start.6) | collective-permute-done | bytes 92192 | tf_op jit(solution)/shard_map/ppermute | solution.py:425
  26.3 0.5 %collective-permute-start.10 = (bf16[72,640]{1,0:T(8,128)(2,1)S(1)}, bf16[72,640]{1,0:T(8,128)(2,1)S(1)}, u32[]{:S(2)}, u32[]{:S(2)}) collective-permute-start(bf16[72,640]{1,0:T(8,128)(2,1)S(1)} %collective-permute-done.6.refs_1_), channel_id=1, source_target_pairs={{0,1},{1,0},{2,3},{3,2},{4,5},{5,4},{6,7},{7,6},{8,9},{9,8},{10,11... | collective-permute-start | bytes 276488 | tf_op jit(solution)/shard_map/ppermute | solution.py:428
  26.8 0.8 %shard_map.58.qb_ref = bf16[512,256]{1,0:T(8,128)(2,1)S(1)} custom-call(bf16[512,1120]{1,0:T(8,128)(2,1)S(1)} %get-tuple-element.29.own_ref, bf16[512,1120]{1,0:T(8,128)(2,1)S(1)} %get-tuple-element.30.other_ref.mod_ref, bf16[1120,256]{1,0:T(8,128)(2,1)S(1)} %bitcast.13, bf16[1120,256]{1,0:T(8,128)(2,1)S(1)} %bitcast.14), custom_call_target="tpu_custom_call" | custom-call | flops 587202560 | bytes 3145728 | tf_op jit(solution)/shard_map/pallas_call | solution.py:472
  27.7 1.8 %collective-permute-start.3 = (bf16[512,256]{1,0:T(8,128)(2,1)S(1)}, bf16[512,256]{1,0:T(8,128)(2,1)S(1)}, u32[]{:S(2)}, u32[]{:S(2)}) collective-permute-start(bf16[512,256]{1,0:T(8,128)(2,1)S(1)} %shard_map.58.qb_ref), channel_id=1, source_target_pairs={{0,2},{2,0},{1,3},{3,1},{4,6},{6,4},{5,7},{7,5},{8,10},{10,8},{9,1... | collective-permute-start | bytes 786440 | tf_op jit(solution)/shard_map/ppermute | solution.py:420
  29.6 0.5 %collective-permute-start.12 = (bf16[72,640]{1,0:T(8,128)(2,1)S(1)}, bf16[72,640]{1,0:T(8,128)(2,1)S(1)}, u32[]{:S(2)}, u32[]{:S(2)}) collective-permute-start(bf16[72,640]{1,0:T(8,128)(2,1)S(1)} %collective-permute-done.8.refs_3_), channel_id=1, source_target_pairs={{0,1},{1,0},{2,3},{3,2},{4,5},{5,4},{6,7},{7,6},{8,9},{9,8},{10,11... | collective-permute-start | bytes 276488 | tf_op jit(solution)/shard_map/ppermute | solution.py:428
  30.1 0.8 %collective-permute-done.11.refs_6_ = bf16[72,640]{1,0:T(8,128)(2,1)S(1)} collective-permute-done((bf16[72,640]{1,0:T(8,128)(2,1)S(1)}, bf16[72,640]{1,0:T(8,128)(2,1)S(1)}, u32[]{:S(2)}, u32[]{:S(2)}) %collective-permute-start.11) | collective-permute-done | bytes 92192 | tf_op jit(solution)/shard_map/ppermute | solution.py:428
  30.8 0.4 shard_map.62.so_far_ref
  31.5 2.6 %shard_map.64 = (f32[1120,512]{1,0:T(8,128)S(1)}, f32[1120,256]{1,0:T(8,128)S(1)}) custom-call(s32[2]{0:T(128)S(1)} %copy-done.2, bf16[512,384]{1,0:T(8,128)(2,1)S(1)} %shard_map.57.after_ref.qa_ref, bf16[512,256]{1,0:T(8,128)(2,1)S(1)} %shard_map.58.qb_ref, f32[72,640]{1,0:T(8,128)S(1)} %get-tuple-element.38.state_ref, bf16[1120,640]{1,0:T(8,128)(2,1)S(1)} %bitcast.9, ...), custom_call_target="tpu_custom_call" | custom-call | flops 734003200 | bytes 4194304 | tf_op jit(solution)/shard_map/pallas_call | solution.py:503
  34.2 2.7 %collective-permute-done.3.refs_1_ = bf16[512,256]{1,0:T(8,128)(2,1)S(1)} collective-permute-done((bf16[512,256]{1,0:T(8,128)(2,1)S(1)}, bf16[512,256]{1,0:T(8,128)(2,1)S(1)}, u32[]{:S(2)}, u32[]{:S(2)}) %collective-permute-start.3) | collective-permute-done | bytes 262176 | tf_op jit(solution)/shard_map/ppermute | solution.py:420
  36.9 1.5 %collective-permute-done.13.refs_2_ = bf16[72,640]{1,0:T(8,128)(2,1)S(1)} collective-permute-done((bf16[72,640]{1,0:T(8,128)(2,1)S(1)}, bf16[72,640]{1,0:T(8,128)(2,1)S(1)}, u32[]{:S(2)}, u32[]{:S(2)}) %collective-permute-start.13) | collective-permute-done | bytes 92192 | tf_op jit(solution)/shard_map/ppermute | solution.py:420
  38.4 2.2 %shard_map.65 = bf16[1120,512]{1,0:T(8,128)(2,1)} custom-call(bf16[512,384]{1,0:T(8,128)(2,1)S(1)} %collective-permute-done.1.refs_0_, bf16[512,256]{1,0:T(8,128)(2,1)S(1)} %collective-permute-done.3.refs_1_, bf16[72,640]{1,0:T(8,128)(2,1)S(1)} %collective-permute-done.13.refs_2_, bf16[1120,640]{1,0:T(8,128)(2,1)S(1)} %bitcast.10, ...), custom_call_target="tpu_custom_call" | custom-call | flops 734003200 | bytes 4194304 | tf_op jit(solution)/shard_map/pallas_call | solution.py:512
  (23 shorter events, 0.8 us)
Async XLA Ops:
  0.0 4.1 %copy-start = (bf16[640,1120]{0,1:T(8,128)(2,1)S(1)}, bf16[640,1120]{0,1:T(8,128)(2,1)}, u32[]{:S(2)}) copy-start(bf16[640,1120]{0,1:T(8,128)(2,1)} %param.9) | copy-start | bytes 4300804
  0.0 4.2 %copy-start.1 = (f32[6,3,2240]{2,1,0:T(4,128)S(1)}, f32[6,3,2240]{2,1,0:T(4,128)}, u32[]{:S(2)}) copy-start(f32[6,3,2240]{2,1,0:T(4,128)} %mods_ref.5) | copy-start | bytes 483844
  0.0 4.2 %copy-start.2 = (s32[2]{0:T(128)S(1)}, s32[2]{0:T(128)}, u32[]{:S(2)}) copy-start(s32[2]{0:T(128)} %img_ref.9) | copy-start | bytes 28
  3.1 8.9 %collective-permute-start.5 = (bf16[1,1120,768]{2,1,0:T(8,128)(2,1)S(1)}, bf16[1,1120,768]{2,1,0:T(8,128)(2,1)S(1)}, u32[]{:S(2)}, u32[]{:S(2)}) collective-permute-start(bf16[1,1120,768]{2,1,0:T(8,128)(2,1)S(1)} %get-tuple-element.27.refs_3_.w0_ref), channel_id=1, source_target_pairs={{0,1},{1,0},{2,3},{3,2},{4,5},{5,4},{6,7},{7,6},{8,9},{9,8},{10,11... | collective-permute-start | bytes 5160968 | tf_op jit(solution)/shard_map/ppermute | solution.py:428
  3.6 10.0 %collective-permute-start.4 = (bf16[1,1120,512]{2,1,0:T(8,128)(2,1)S(1)}, bf16[1,1120,512]{2,1,0:T(8,128)(2,1)S(1)}, u32[]{:S(2)}, u32[]{:S(2)}) collective-permute-start(bf16[1,1120,512]{2,1,0:T(8,128)(2,1)S(1)} %get-tuple-element.28.refs_4_.w1_ref), channel_id=1, source_target_pairs={{0,1},{1,0},{2,3},{3,2},{4,5},{5,4},{6,7},{7,6},{8,9},{9,8},{10,11... | collective-permute-start | bytes 3440648 | tf_op jit(solution)/shard_map/ppermute | solution.py:428
  3.7 6.0 %collective-permute-start = (bf16[1,1120,384]{2,1,0:T(8,128)(2,1)S(1)}, bf16[1,1120,384]{2,1,0:T(8,128)(2,1)S(1)}, u32[]{:S(2)}, u32[]{:S(2)}) collective-permute-start(bf16[1,1120,384]{2,1,0:T(8,128)(2,1)S(1)} %get-tuple-element.26.refs_2_), channel_id=1, source_target_pairs={{0,1},{1,0},{2,3},{3,2},{4,5},{5,4},{6,7},{7,6},{8,9},{9,8},{10,11... | collective-permute-start | bytes 2580488 | tf_op jit(solution)/shard_map/ppermute | solution.py:428
  4.1 27.4 %collective-permute-start.14 = (bf16[1120,640]{1,0:T(8,128)(2,1)S(1)}, bf16[1120,640]{1,0:T(8,128)(2,1)S(1)}, u32[]{:S(2)}, u32[]{:S(2)}) collective-permute-start(bf16[1120,640]{1,0:T(8,128)(2,1)S(1)} %bitcast.8), channel_id=1, source_target_pairs={{0,1},{1,0},{2,3},{3,2},{4,5},{5,4},{6,7},{7,6},{8,9},{9,8},{10,11... | collective-permute-start | bytes 4300808 | tf_op jit(solution)/shard_map/ppermute | solution.py:428
  6.5 15.1 %collective-permute-start.2 = (bf16[1,1120,256]{2,1,0:T(8,128)(2,1)S(1)}, bf16[1,1120,256]{2,1,0:T(8,128)(2,1)S(1)}, u32[]{:S(2)}, u32[]{:S(2)}) collective-permute-start(bf16[1,1120,256]{2,1,0:T(8,128)(2,1)S(1)} %get-tuple-element.32), channel_id=1, source_target_pairs={{0,1},{1,0},{2,3},{3,2},{4,5},{5,4},{6,7},{7,6},{8,9},{9,8},{10,11... | collective-permute-start | bytes 1720328 | tf_op jit(solution)/shard_map/ppermute | solution.py:428
  14.8 11.5 %collective-permute-start.6 = (bf16[72,640]{1,0:T(8,128)(2,1)S(1)}, bf16[72,640]{1,0:T(8,128)(2,1)S(1)}, u32[]{:S(2)}, u32[]{:S(2)}) collective-permute-start(bf16[72,640]{1,0:T(8,128)(2,1)S(1)} %shard_map.61.refs_0_.own_ref), channel_id=1, source_target_pairs={{0,8},{4,12},{8,0},{12,4},{1,9},{5,13},{9,1},{13,5},{2,10},{6,14},... | collective-permute-start | bytes 276488 | tf_op jit(solution)/shard_map/ppermute | solution.py:425
  18.8 7.5 %collective-permute-start.7 = (bf16[72,640]{1,0:T(8,128)(2,1)S(1)}, bf16[72,640]{1,0:T(8,128)(2,1)S(1)}, u32[]{:S(2)}, u32[]{:S(2)}) collective-permute-start(bf16[72,640]{1,0:T(8,128)(2,1)S(1)} %shard_map.61.refs_0_.own_ref), channel_id=1, source_target_pairs={{0,12},{4,8},{8,4},{12,0},{1,13},{5,9},{9,5},{13,1},{2,14},{6,10},... | collective-permute-start | bytes 276488 | tf_op jit(solution)/shard_map/ppermute | solution.py:425
  20.2 16.7 %collective-permute-start.1 = (bf16[512,384]{1,0:T(8,128)(2,1)S(1)}, bf16[512,384]{1,0:T(8,128)(2,1)S(1)}, u32[]{:S(2)}, u32[]{:S(2)}) collective-permute-start(bf16[512,384]{1,0:T(8,128)(2,1)S(1)} %shard_map.57.after_ref.qa_ref), channel_id=1, source_target_pairs={{0,2},{2,0},{1,3},{3,1},{4,6},{6,4},{5,7},{7,5},{8,10},{10,8},{9,1... | collective-permute-start | bytes 1179656 | tf_op jit(solution)/shard_map/ppermute | solution.py:420
  21.7 6.0 %collective-permute-start.8 = (bf16[72,640]{1,0:T(8,128)(2,1)S(1)}, bf16[72,640]{1,0:T(8,128)(2,1)S(1)}, u32[]{:S(2)}, u32[]{:S(2)}) collective-permute-start(bf16[72,640]{1,0:T(8,128)(2,1)S(1)} %shard_map.61.refs_0_.own_ref), channel_id=1, source_target_pairs={{0,4},{4,0},{8,12},{12,8},{1,5},{5,1},{9,13},{13,9},{2,6},{6,2},{1... | collective-permute-start | bytes 276488 | tf_op jit(solution)/shard_map/ppermute | solution.py:425
  26.3 3.3 %collective-permute-start.9 = (bf16[72,640]{1,0:T(8,128)(2,1)S(1)}, bf16[72,640]{1,0:T(8,128)(2,1)S(1)}, u32[]{:S(2)}, u32[]{:S(2)}) collective-permute-start(bf16[72,640]{1,0:T(8,128)(2,1)S(1)} %shard_map.61.refs_0_.own_ref), channel_id=1, source_target_pairs={{0,1},{1,0},{2,3},{3,2},{4,5},{5,4},{6,7},{7,6},{8,9},{9,8},{10,11... | collective-permute-start | bytes 276488 | tf_op jit(solution)/shard_map/ppermute | solution.py:428
  26.3 3.3 %collective-permute-start.10 = (bf16[72,640]{1,0:T(8,128)(2,1)S(1)}, bf16[72,640]{1,0:T(8,128)(2,1)S(1)}, u32[]{:S(2)}, u32[]{:S(2)}) collective-permute-start(bf16[72,640]{1,0:T(8,128)(2,1)S(1)} %collective-permute-done.6.refs_1_), channel_id=1, source_target_pairs={{0,1},{1,0},{2,3},{3,2},{4,5},{5,4},{6,7},{7,6},{8,9},{9,8},{10,11... | collective-permute-start | bytes 276488 | tf_op jit(solution)/shard_map/ppermute | solution.py:428
  27.7 9.2 %collective-permute-start.3 = (bf16[512,256]{1,0:T(8,128)(2,1)S(1)}, bf16[512,256]{1,0:T(8,128)(2,1)S(1)}, u32[]{:S(2)}, u32[]{:S(2)}) collective-permute-start(bf16[512,256]{1,0:T(8,128)(2,1)S(1)} %shard_map.58.qb_ref), channel_id=1, source_target_pairs={{0,2},{2,0},{1,3},{3,1},{4,6},{6,4},{5,7},{7,5},{8,10},{10,8},{9,1... | collective-permute-start | bytes 786440 | tf_op jit(solution)/shard_map/ppermute | solution.py:420
  29.5 1.3 %collective-permute-start.11 = (bf16[72,640]{1,0:T(8,128)(2,1)S(1)}, bf16[72,640]{1,0:T(8,128)(2,1)S(1)}, u32[]{:S(2)}, u32[]{:S(2)}) collective-permute-start(bf16[72,640]{1,0:T(8,128)(2,1)S(1)} %collective-permute-done.7.refs_2_), channel_id=1, source_target_pairs={{0,1},{1,0},{2,3},{3,2},{4,5},{5,4},{6,7},{7,6},{8,9},{9,8},{10,11... | collective-permute-start | bytes 276488 | tf_op jit(solution)/shard_map/ppermute | solution.py:428
  29.6 1.6 %collective-permute-start.12 = (bf16[72,640]{1,0:T(8,128)(2,1)S(1)}, bf16[72,640]{1,0:T(8,128)(2,1)S(1)}, u32[]{:S(2)}, u32[]{:S(2)}) collective-permute-start(bf16[72,640]{1,0:T(8,128)(2,1)S(1)} %collective-permute-done.8.refs_3_), channel_id=1, source_target_pairs={{0,1},{1,0},{2,3},{3,2},{4,5},{5,4},{6,7},{7,6},{8,9},{9,8},{10,11... | collective-permute-start | bytes 276488 | tf_op jit(solution)/shard_map/ppermute | solution.py:428
  31.3 7.1 %collective-permute-start.13 = (bf16[72,640]{1,0:T(8,128)(2,1)S(1)}, bf16[72,640]{1,0:T(8,128)(2,1)S(1)}, u32[]{:S(2)}, u32[]{:S(2)}) collective-permute-start(bf16[72,640]{1,0:T(8,128)(2,1)S(1)} %get-tuple-element.37), channel_id=1, source_target_pairs={{0,2},{2,0},{1,3},{3,1},{4,6},{6,4},{5,7},{7,5},{8,10},{10,8},{9,1... | collective-permute-start | bytes 276488 | tf_op jit(solution)/shard_map/ppermute | solution.py:420
